TPU v7x, 32 devices: a whole 2x2x4 slice. The times are simulated.
32 devices in a mesh: segment: 4 (over y, core), vol: 8 (over z, x).
Axes of the slice: x: 2, y: 2, z: 4, core: 2. Of those that a mesh axis runs over, the one named last changes fastest.
Arguments:
- cotangent: bfloat16 [64, 32, 256], P(None, 'vol'), may hold values from -6 to 6
- labels: int32 [32, 256], P('vol'), may hold values from 0 to 2
- class_weight: float32 [3], replicated, may hold values from 0.25 to 2
- inputs: bfloat16 [4, 64, 32, 256], P('segment', None, 'vol'), may hold values from -6 to 6
- fine_pre: bfloat16 [4, 64, 32, 256], P('segment', None, 'vol'), may hold values from -6 to 6
- pooled: bfloat16 [4, 64, 8, 128], P('segment', None, 'vol'), may hold values from -6 to 6
- coarse_pre: bfloat16 [4, 64, 8, 128], P('segment', None, 'vol'), may hold values from -6 to 6
- fine_filters: bfloat16 [4, 27, 64, 64], P('segment'), may hold values from -0.15625 to 0.15625
- coarse_filters: bfloat16 [4, 27, 64, 64], P('segment'), may hold values from -0.15625 to 0.15625
Outputs:
- input_grads: bfloat16 [4, 64, 32, 256], P('segment', None, 'vol')
- fine_filter_grads: float32 [4, 27, 64, 64], P('segment')
- coarse_filter_grads: float32 [4, 27, 64, 64], P('segment')
Inputs may be any that keep to these rules, and one draw needn't show every extreme that they name: `labels`: 0 is background, 1 fault, 2 horizon.
All inputs are finite; a program needn't handle non-finite values.
Results may differ from a plain program's by a relative error of at most 0.02.
Values may be sent and summed in bfloat16 or wider, within the bound.
A program may use at most 64 MiB of HBM per device.

v0:
```python
import math

import jax
import jax.numpy as jnp
from jax import lax
from jax.sharding import PartitionSpec as P

XL = 16


def shortened(array):
    return jax.tree.map(lambda a: a.astype(jnp.bfloat16) if a.dtype == jnp.float32 else a, array)


def padded_2(block, sides, width):
    for axis, dim in sides:
        count = lax.axis_size(axis)
        forward = [(i, i + 1) for i in range(count - 1)]
        backward = [(target, source) for source, target in forward]
        low = lax.ppermute(
            lax.slice_in_dim(block, block.shape[dim] - width, None, axis=dim), axis, forward
        )
        high = lax.ppermute(lax.slice_in_dim(block, 0, width, axis=dim), axis, backward)
        block = jnp.concatenate([low, block, high], axis=dim)
    return block


def from_behind(array, axis, by):
    devices = lax.axis_size(axis)
    pairs = [(i, i + by) for i in range(devices) if 0 <= i + by < devices]
    return lax.ppermute(array, axis, pairs)


def plane_shift(volume, columns, row_step, col_step):
    length = volume.shape[-1]
    offset = row_step * columns + col_step
    margin = columns + 1
    widths = [(0, 0)] * (volume.ndim - 1) + [(margin, margin)]
    padded = jnp.pad(volume, widths)
    shifted = lax.slice_in_dim(
        padded, margin - offset, margin - offset + length, axis=volume.ndim - 1
    )
    column = lax.broadcasted_iota(jnp.int32, (length,), 0) % columns
    inside = (column >= col_step) & (column < columns + col_step)
    return jnp.where(inside, shifted, jnp.zeros_like(shifted))


def tap_pieces(padded, columns):
    slab_count = padded.shape[1] - 2
    pieces = {}
    for middle_tap in range(3):
        for inner_tap in range(3):
            moved_plane = plane_shift(padded, columns, middle_tap - 1, inner_tap - 1)
            for outer_tap in range(3):
                pieces[outer_tap, middle_tap, inner_tap] = lax.slice_in_dim(
                    moved_plane, 2 - outer_tap, 2 - outer_tap + slab_count, axis=1
                )
    return pieces


def kernel_view(weights):
    kernel = weights.reshape(3, 3, 3, weights.shape[1], weights.shape[2])
    return kernel


def back_sum(pieces, weights):
    kernel = kernel_view(weights)
    summed = None
    for tap_key in sorted(pieces):
        term = jnp.einsum(
            "io,orp->irp", kernel[tap_key], pieces[tap_key], preferred_element_type=jnp.float32
        )
        summed = term if summed is None else summed + term
    return summed


def filter_grid(pieces, saved_local):
    outer_list = []
    for outer_tap in range(3):
        middle_list = []
        for middle_tap in range(3):
            inner_list = []
            for inner_tap in range(3):
                inner_list.append(
                    jnp.einsum(
                        "irp,orp->io",
                        saved_local,
                        pieces[outer_tap, middle_tap, inner_tap],
                        preferred_element_type=jnp.float32,
                    )
                )
            middle_list.append(jnp.stack(inner_list))
        outer_list.append(jnp.stack(middle_list))
    tap_grid = jnp.stack(outer_list)
    return tap_grid.reshape(27, tap_grid.shape[3], tap_grid.shape[4])


def edge_rims(payload):
    return padded_2(shortened(payload), (("vol", 1),), 1).astype(payload.dtype)


def to_depth(payload, half_cols):
    channels = payload.shape[0]
    full_depth = payload.shape[2] // half_cols
    shaped = payload.reshape(channels, full_depth, 1, half_cols)
    moved = lax.all_to_all(
        shortened(shaped), "vol", split_axis=1, concat_axis=2, tiled=True
    ).astype(shaped.dtype)
    return moved.reshape(channels, moved.shape[1], moved.shape[2] * half_cols)


def pool_sum(grad_wide, half_depth, half_rows, half_cols):
    channels = grad_wide.shape[0]
    blocks = grad_wide.reshape(channels, half_depth, 2, half_rows, 2, half_cols, 2)
    return blocks.sum(axis=(2, 4, 6)).reshape(channels, half_depth, half_rows * half_cols)


def spread_up(coarse_back, half_depth, half_rows, half_cols):
    channels = coarse_back.shape[0]
    widened = coarse_back.astype(jnp.float32).reshape(
        channels, half_depth, 1, half_rows, 1, half_cols, 1
    )
    widened = jnp.broadcast_to(widened, (channels, half_depth, 2, half_rows, 2, half_cols, 2))
    return widened.reshape(channels, 2 * half_depth, 8 * half_rows * half_cols // 2)


def on_device(
    cotangent,
    labels,
    class_weight,
    inputs,
    fine_pre,
    pooled,
    coarse_pre,
    fine_filters,
    coarse_filters,
):
    segments = lax.axis_size("segment")
    vol_count = lax.axis_size("vol")
    position = lax.axis_index("segment")
    channels = inputs.shape[1]
    depth_len = inputs.shape[2]
    plane_len = inputs.shape[3]
    inline_len = plane_len // XL
    half_cols = XL // 2
    half_depth = depth_len // 2
    half_inline = inline_len // 2
    cell_weight = jnp.zeros(labels.shape, jnp.float32)
    for class_index in range(class_weight.shape[0]):
        cell_weight = cell_weight + jnp.where(labels == class_index, class_weight[class_index], 0.0)
    seed_grad = (cotangent.astype(jnp.float32) * cell_weight[None]).astype(jnp.bfloat16)
    coarse_pair = jnp.concatenate([pooled[0], coarse_pre[0]], axis=0)
    stacked = to_depth(coarse_pair, half_cols)
    coarse_saved = stacked[:channels]
    coarse_mask = stacked[channels:] > 0
    saved_input = inputs[0]
    fine_mask = fine_pre[0] > 0
    fine_kernel = fine_filters[0]
    coarse_kernel = coarse_filters[0]
    incoming = jnp.where(position == segments - 1, seed_grad, jnp.zeros_like(seed_grad))

    def advance(turn_index, carry):
        gradient, grad_keep, fine_keep, coarse_keep = carry
        grad_wide = gradient.astype(jnp.float32)
        coarse_grad = pool_sum(grad_wide, half_depth, half_inline, half_cols).astype(jnp.bfloat16)
        coarse_gz = jnp.where(coarse_mask, coarse_grad, jnp.zeros_like(coarse_grad))
        coarse_pad = edge_rims(coarse_gz)
        coarse_back = back_sum(tap_pieces(coarse_pad, half_cols), coarse_kernel).astype(
            jnp.bfloat16
        )
        fine_grad = grad_wide + 0.125 * spread_up(coarse_back, half_depth, half_inline, half_cols)
        fine_gz = jnp.where(fine_mask, fine_grad, 0.0).astype(jnp.bfloat16)
        fine_pad = edge_rims(fine_gz)
        out_grad = (grad_wide + back_sum(tap_pieces(fine_pad, XL), fine_kernel)).astype(
            jnp.bfloat16
        )
        active = turn_index == segments - 1 - position
        grad_keep = jnp.where(active, out_grad, grad_keep)
        fine_keep = jnp.where(active, fine_pad, fine_keep)
        coarse_keep = jnp.where(active, coarse_pad, coarse_keep)
        passed = from_behind(out_grad, "segment", -1)
        return (passed, grad_keep, fine_keep, coarse_keep)

    start = (
        incoming,
        jnp.zeros(saved_input.shape, jnp.bfloat16),
        jnp.zeros((channels, depth_len + 2, plane_len), jnp.bfloat16),
        jnp.zeros((channels, coarse_saved.shape[1] + 2, coarse_saved.shape[2]), jnp.bfloat16),
    )
    finished = lax.fori_loop(0, segments, advance, start)
    grad_result = finished[1]
    fine_local = filter_grid(tap_pieces(finished[2], XL), saved_input)
    coarse_local = filter_grid(tap_pieces(finished[3], half_cols), coarse_saved)
    fine_total, coarse_total = (
        lax.psum(fine_local.astype(jnp.bfloat16), "vol").astype(jnp.float32),
        lax.psum(coarse_local.astype(jnp.bfloat16), "vol").astype(jnp.float32),
    )
    fine_cells = depth_len * vol_count * plane_len
    fine_total = fine_total * (1.0 / math.sqrt(fine_cells))
    coarse_total = coarse_total * (1.0 / math.sqrt(fine_cells // 8))
    return (grad_result[None], fine_total[None], coarse_total[None])


def solution(mesh):
    return jax.shard_map(
        on_device,
        mesh=mesh,
        in_specs=(
            P(None, "vol", None),
            P("vol", None),
            P(),
            P("segment", None, "vol", None),
            P("segment", None, "vol", None),
            P("segment", None, "vol", None),
            P("segment", None, "vol", None),
            P("segment", None, None, None),
            P("segment", None, None, None),
        ),
        out_specs=(
            P("segment", None, "vol", None),
            P("segment", None, None, None),
            P("segment", None, None, None),
        ),
        check_vma=False,
    )
```

profile of v0, /device:TPU:0, one launch (start us, length us, event | category | flops | bytes accessed | tf_op | source)
XLA Modules:
  0.0 262.4 jit_solution(14999166391219055556)
XLA Ops:
  9.0 7.3 %all-to-all-start = ((bf16[128,16,1,8]{0,3,2,1:T(8,128)(2,1)}), bf16[128,16,1,8]{0,3,2,1:T(8,128)(2,1)S(1)}, u32[]{:S(2)}, u32[]{:S(2)}) async-start(bf16[128,16,1,8]{0,3,2,1:T(8,128)(2,1)} %maximum_bitcast_fusion.24), calls=%async_computation | async-start | bytes 65536 | tf_op jit(solution)/shard_map/all_to_all | solution.py:106
  16.4 1.4 fusion.382
  17.9 2.7 %select_add_fusion = f32[4,256]{1,0:T(4,128)S(1)} fusion(s32[4,256]{1,0:T(4,128)} %param.12, f32[]{:T(128)} %bitcast.2, f32[]{:T(128)} %bitcast.1, f32[]{:T(128)} %bitcast), kind=kLoop, calls=%fused_computation.494 | loop fusion | flops 8192 | bytes 8204 | tf_op jit(solution)/shard_map/add | solution.py:150
  20.6 2.4 all-to-all-done
  23.0 130.6 %while.23 = (s32[]{:T(128)}, bf16[64,4,256]{2,0,1:T(8,128)(2,1)S(1)}, bf16[64,4,256]{2,0,1:T(8,128)(2,1)S(1)}, bf16[64,6,256]{2,0,1:T(8,128)(2,1)S(1)}, bf16[64,...) while((s32[]{:T(128)}, ...), condition=%wide.region_2.3_spmd.clone, body=%wide.region_0.2_spmd.clone.sunk | while | flops 259488704 | bytes 29859644 | solution.py:190
  24.9 4.5 %collective-permute-start.1 = (bf16[64,1,64]{0,2,1:T(8,128)(2,1)S(1)}, bf16[64,1,64]{0,2,1:T(8,128)(2,1)S(1)}, u32[]{:S(2)}, u32[]{:S(2)}) collective-permute-start(bf16[64,1,64]{0,2,1:T(8,128)(2,1)S(1)} %get-tuple-element.480), channel_id=1, source_target_pairs={{0,1},{1,2},{2,3},{3,4},{4,5},{5,6},{6,7},{8,9},{9,10},{10,11},{11... | collective-permute-start | bytes 24584 | tf_op jit(solution)/shard_map/while/body/eval_jaxpr/ppermute | solution.py:20
  37.9 4.8 %collective-permute-start.3 = (bf16[64,1,256]{2,0,1:T(8,128)(2,1)S(1)}, bf16[64,1,256]{2,0,1:T(8,128)(2,1)S(1)}, u32[]{:S(2)}, u32[]{:S(2)}) collective-permute-start(bf16[64,1,256]{2,0,1:T(8,128)(2,1)S(1)} %get-tuple-element.483), channel_id=1, source_target_pairs={{0,1},{1,2},{2,3},{3,4},{4,5},{5,6},{6,7},{8,9},{9,10},{10,11},{11... | collective-permute-start | bytes 98312 | tf_op jit(solution)/shard_map/while/body/eval_jaxpr/ppermute | solution.py:20
  42.8 1.6 collective-permute-done.3
  51.5 1.9 collective-permute-done.4
  55.3 5.4 %collective-permute-start.1 = (bf16[64,1,64]{0,2,1:T(8,128)(2,1)S(1)}, bf16[64,1,64]{0,2,1:T(8,128)(2,1)S(1)}, u32[]{:S(2)}, u32[]{:S(2)}) collective-permute-start(bf16[64,1,64]{0,2,1:T(8,128)(2,1)S(1)} %get-tuple-element.480), channel_id=1, source_target_pairs={{0,1},{1,2},{2,3},{3,4},{4,5},{5,6},{6,7},{8,9},{9,10},{10,11},{11... | collective-permute-start | bytes 24584 | tf_op jit(solution)/shard_map/while/body/eval_jaxpr/ppermute | solution.py:20
  69.2 5.8 %collective-permute-start.3 = (bf16[64,1,256]{2,0,1:T(8,128)(2,1)S(1)}, bf16[64,1,256]{2,0,1:T(8,128)(2,1)S(1)}, u32[]{:S(2)}, u32[]{:S(2)}) collective-permute-start(bf16[64,1,256]{2,0,1:T(8,128)(2,1)S(1)} %get-tuple-element.483), channel_id=1, source_target_pairs={{0,1},{1,2},{2,3},{3,4},{4,5},{5,6},{6,7},{8,9},{9,10},{10,11},{11... | collective-permute-start | bytes 98312 | tf_op jit(solution)/shard_map/while/body/eval_jaxpr/ppermute | solution.py:20
  75.0 1.6 collective-permute-done.3
  83.6 2.7 %collective-permute-done.4 = bf16[64,4,256]{2,0,1:T(8,128)(2,1)S(1)} collective-permute-done((bf16[64,4,256]{2,0,1:T(8,128)(2,1)S(1)}, bf16[64,4,256]{2,0,1:T(8,128)(2,1)S(1)}, u32[]{:S(2)}, u32[]{:S(2)}) %collective-permute-start.4) | collective-permute-done | bytes 131104 | tf_op jit(solution)/shard_map/while/body/eval_jaxpr/ppermute | solution.py:31
  88.2 5.4 %collective-permute-start.1 = (bf16[64,1,64]{0,2,1:T(8,128)(2,1)S(1)}, bf16[64,1,64]{0,2,1:T(8,128)(2,1)S(1)}, u32[]{:S(2)}, u32[]{:S(2)}) collective-permute-start(bf16[64,1,64]{0,2,1:T(8,128)(2,1)S(1)} %get-tuple-element.480), channel_id=1, source_target_pairs={{0,1},{1,2},{2,3},{3,4},{4,5},{5,6},{6,7},{8,9},{9,10},{10,11},{11... | collective-permute-start | bytes 24584 | tf_op jit(solution)/shard_map/while/body/eval_jaxpr/ppermute | solution.py:20
  93.7 1.4 collective-permute-done.1
  102.1 5.5 %collective-permute-start.3 = (bf16[64,1,256]{2,0,1:T(8,128)(2,1)S(1)}, bf16[64,1,256]{2,0,1:T(8,128)(2,1)S(1)}, u32[]{:S(2)}, u32[]{:S(2)}) collective-permute-start(bf16[64,1,256]{2,0,1:T(8,128)(2,1)S(1)} %get-tuple-element.483), channel_id=1, source_target_pairs={{0,1},{1,2},{2,3},{3,4},{4,5},{5,6},{6,7},{8,9},{9,10},{10,11},{11... | collective-permute-start | bytes 98312 | tf_op jit(solution)/shard_map/while/body/eval_jaxpr/ppermute | solution.py:20
  107.6 1.6 collective-permute-done.3
  116.3 3.7 %collective-permute-done.4 = bf16[64,4,256]{2,0,1:T(8,128)(2,1)S(1)} collective-permute-done((bf16[64,4,256]{2,0,1:T(8,128)(2,1)S(1)}, bf16[64,4,256]{2,0,1:T(8,128)(2,1)S(1)}, u32[]{:S(2)}, u32[]{:S(2)}) %collective-permute-start.4) | collective-permute-done | bytes 131104 | tf_op jit(solution)/shard_map/while/body/eval_jaxpr/ppermute | solution.py:31
  121.8 5.4 %collective-permute-start.1 = (bf16[64,1,64]{0,2,1:T(8,128)(2,1)S(1)}, bf16[64,1,64]{0,2,1:T(8,128)(2,1)S(1)}, u32[]{:S(2)}, u32[]{:S(2)}) collective-permute-start(bf16[64,1,64]{0,2,1:T(8,128)(2,1)S(1)} %get-tuple-element.480), channel_id=1, source_target_pairs={{0,1},{1,2},{2,3},{3,4},{4,5},{5,6},{6,7},{8,9},{9,10},{10,11},{11... | collective-permute-start | bytes 24584 | tf_op jit(solution)/shard_map/while/body/eval_jaxpr/ppermute | solution.py:20
  135.7 5.5 %collective-permute-start.3 = (bf16[64,1,256]{2,0,1:T(8,128)(2,1)S(1)}, bf16[64,1,256]{2,0,1:T(8,128)(2,1)S(1)}, u32[]{:S(2)}, u32[]{:S(2)}) collective-permute-start(bf16[64,1,256]{2,0,1:T(8,128)(2,1)S(1)} %get-tuple-element.483), channel_id=1, source_target_pairs={{0,1},{1,2},{2,3},{3,4},{4,5},{5,6},{6,7},{8,9},{9,10},{10,11},{11... | collective-permute-start | bytes 98312 | tf_op jit(solution)/shard_map/while/body/eval_jaxpr/ppermute | solution.py:20
  141.2 1.6 collective-permute-done.3
  149.9 3.7 %collective-permute-done.4 = bf16[64,4,256]{2,0,1:T(8,128)(2,1)S(1)} collective-permute-done((bf16[64,4,256]{2,0,1:T(8,128)(2,1)S(1)}, bf16[64,4,256]{2,0,1:T(8,128)(2,1)S(1)}, u32[]{:S(2)}, u32[]{:S(2)}) %collective-permute-start.4) | collective-permute-done | bytes 131104 | tf_op jit(solution)/shard_map/while/body/eval_jaxpr/ppermute | solution.py:31
  168.5 84.0 %all-reduce.7.cloned.1.call-done = (bf16[27,64,64]{2,1,0:T(8,128)(2,1)}, bf16[27,64,64]{2,1,0:T(8,128)(2,1)}) async-done(((bf16[27,64,64]{2,1,0:T(8,128)(2,1)}, bf16[27,64,64]{2,1,0:T(8,128)(2,1)}), (bf16[27,64,64]{2,1,0:T(8,128)(2,1)}, bf16[27,64,64]{2,1,0:T(8,128)(2,1)})) %all-reduce.7.cloned.1.call-update) | async-done | bytes 442384 | tf_op jit(solution)/shard_map/psum | solution.py:195
  252.5 2.1 multiply_bitcast_fusion
  (421 shorter events, 84.3 us)
Async XLA Ops:
  7.2 151.7 %copy-start = (bf16[1,64,4,256]{3,2,1,0:T(4,128)(2,1)S(1)}, bf16[1,64,4,256]{3,2,1,0:T(4,128)(2,1)}, u32[]{:S(2)}) copy-start(bf16[1,64,4,256]{3,2,1,0:T(4,128)(2,1)} %param.14) | copy-start | bytes 393220
  7.2 15.8 %copy-start.1 = (bf16[1,27,64,64]{3,2,1,0:T(8,128)(2,1)S(1)}, bf16[1,27,64,64]{3,2,1,0:T(8,128)(2,1)}, u32[]{:S(2)}) copy-start(bf16[1,27,64,64]{3,2,1,0:T(8,128)(2,1)} %param.19) | copy-start | bytes 663556
  9.0 14.0 %all-to-all-start = ((bf16[128,16,1,8]{0,3,2,1:T(8,128)(2,1)}), bf16[128,16,1,8]{0,3,2,1:T(8,128)(2,1)S(1)}, u32[]{:S(2)}, u32[]{:S(2)}) async-start(bf16[128,16,1,8]{0,3,2,1:T(8,128)(2,1)} %maximum_bitcast_fusion.24), calls=%async_computation | async-start | bytes 65536 | tf_op jit(solution)/shard_map/all_to_all | solution.py:106
  16.2 236.3 %all-reduce.7.cloned.1.call-start = ((), (), s32[]{:S(2)}) async-start(), calls=%async_computation.1 | async-start | bytes 1769472 | tf_op jit(solution)/shard_map/psum | solution.py:195
  23.6 5.9 %collective-permute-start = (bf16[64,1,64]{0,2,1:T(8,128)(2,1)S(1)}, bf16[64,1,64]{0,2,1:T(8,128)(2,1)S(1)}, u32[]{:S(2)}, u32[]{:S(2)}) collective-permute-start(bf16[64,1,64]{0,2,1:T(8,128)(2,1)S(1)} %get-tuple-element.479), channel_id=1, source_target_pairs={{1,0},{2,1},{3,2},{4,3},{5,4},{6,5},{7,6},{9,8},{10,9},{11,10},{12... | collective-permute-start | bytes 24584 | tf_op jit(solution)/shard_map/while/body/eval_jaxpr/ppermute | solution.py:23
  24.9 6.0 %collective-permute-start.1 = (bf16[64,1,64]{0,2,1:T(8,128)(2,1)S(1)}, bf16[64,1,64]{0,2,1:T(8,128)(2,1)S(1)}, u32[]{:S(2)}, u32[]{:S(2)}) collective-permute-start(bf16[64,1,64]{0,2,1:T(8,128)(2,1)S(1)} %get-tuple-element.480), channel_id=1, source_target_pairs={{0,1},{1,2},{2,3},{3,4},{4,5},{5,6},{6,7},{8,9},{9,10},{10,11},{11... | collective-permute-start | bytes 24584 | tf_op jit(solution)/shard_map/while/body/eval_jaxpr/ppermute | solution.py:20
  36.6 6.2 %collective-permute-start.2 = (bf16[64,1,256]{2,0,1:T(8,128)(2,1)S(1)}, bf16[64,1,256]{2,0,1:T(8,128)(2,1)S(1)}, u32[]{:S(2)}, u32[]{:S(2)}) collective-permute-start(bf16[64,1,256]{2,0,1:T(8,128)(2,1)S(1)} %get-tuple-element.482), channel_id=1, source_target_pairs={{1,0},{2,1},{3,2},{4,3},{5,4},{6,5},{7,6},{9,8},{10,9},{11,10},{12... | collective-permute-start | bytes 98312 | tf_op jit(solution)/shard_map/while/body/eval_jaxpr/ppermute | solution.py:23
  37.9 6.4 %collective-permute-start.3 = (bf16[64,1,256]{2,0,1:T(8,128)(2,1)S(1)}, bf16[64,1,256]{2,0,1:T(8,128)(2,1)S(1)}, u32[]{:S(2)}, u32[]{:S(2)}) collective-permute-start(bf16[64,1,256]{2,0,1:T(8,128)(2,1)S(1)} %get-tuple-element.483), channel_id=1, source_target_pairs={{0,1},{1,2},{2,3},{3,4},{4,5},{5,6},{6,7},{8,9},{9,10},{10,11},{11... | collective-permute-start | bytes 98312 | tf_op jit(solution)/shard_map/while/body/eval_jaxpr/ppermute | solution.py:20
  50.2 3.2 %collective-permute-start.4 = (bf16[64,4,256]{2,0,1:T(8,128)(2,1)S(1)}, bf16[64,4,256]{2,0,1:T(8,128)(2,1)S(1)}, u32[]{:S(2)}, u32[]{:S(2)}) collective-permute-start(bf16[64,4,256]{2,0,1:T(8,128)(2,1)S(1)} %get-tuple-element.496), channel_id=1, source_target_pairs={{8,0},{16,8},{24,16},{9,1},{17,9},{25,17},{10,2},{18,10},{26,18},{... | collective-permute-start | bytes 393224 | tf_op jit(solution)/shard_map/while/body/eval_jaxpr/ppermute | solution.py:31
  54.0 6.8 %collective-permute-start = (bf16[64,1,64]{0,2,1:T(8,128)(2,1)S(1)}, bf16[64,1,64]{0,2,1:T(8,128)(2,1)S(1)}, u32[]{:S(2)}, u32[]{:S(2)}) collective-permute-start(bf16[64,1,64]{0,2,1:T(8,128)(2,1)S(1)} %get-tuple-element.479), channel_id=1, source_target_pairs={{1,0},{2,1},{3,2},{4,3},{5,4},{6,5},{7,6},{9,8},{10,9},{11,10},{12... | collective-permute-start | bytes 24584 | tf_op jit(solution)/shard_map/while/body/eval_jaxpr/ppermute | solution.py:23
  55.3 6.9 %collective-permute-start.1 = (bf16[64,1,64]{0,2,1:T(8,128)(2,1)S(1)}, bf16[64,1,64]{0,2,1:T(8,128)(2,1)S(1)}, u32[]{:S(2)}, u32[]{:S(2)}) collective-permute-start(bf16[64,1,64]{0,2,1:T(8,128)(2,1)S(1)} %get-tuple-element.480), channel_id=1, source_target_pairs={{0,1},{1,2},{2,3},{3,4},{4,5},{5,6},{6,7},{8,9},{9,10},{10,11},{11... | collective-permute-start | bytes 24584 | tf_op jit(solution)/shard_map/while/body/eval_jaxpr/ppermute | solution.py:20
  67.9 7.1 %collective-permute-start.2 = (bf16[64,1,256]{2,0,1:T(8,128)(2,1)S(1)}, bf16[64,1,256]{2,0,1:T(8,128)(2,1)S(1)}, u32[]{:S(2)}, u32[]{:S(2)}) collective-permute-start(bf16[64,1,256]{2,0,1:T(8,128)(2,1)S(1)} %get-tuple-element.482), channel_id=1, source_target_pairs={{1,0},{2,1},{3,2},{4,3},{5,4},{6,5},{7,6},{9,8},{10,9},{11,10},{12... | collective-permute-start | bytes 98312 | tf_op jit(solution)/shard_map/while/body/eval_jaxpr/ppermute | solution.py:23
  69.2 7.3 %collective-permute-start.3 = (bf16[64,1,256]{2,0,1:T(8,128)(2,1)S(1)}, bf16[64,1,256]{2,0,1:T(8,128)(2,1)S(1)}, u32[]{:S(2)}, u32[]{:S(2)}) collective-permute-start(bf16[64,1,256]{2,0,1:T(8,128)(2,1)S(1)} %get-tuple-element.483), channel_id=1, source_target_pairs={{0,1},{1,2},{2,3},{3,4},{4,5},{5,6},{6,7},{8,9},{9,10},{10,11},{11... | collective-permute-start | bytes 98312 | tf_op jit(solution)/shard_map/while/body/eval_jaxpr/ppermute | solution.py:20
  82.3 4.0 %collective-permute-start.4 = (bf16[64,4,256]{2,0,1:T(8,128)(2,1)S(1)}, bf16[64,4,256]{2,0,1:T(8,128)(2,1)S(1)}, u32[]{:S(2)}, u32[]{:S(2)}) collective-permute-start(bf16[64,4,256]{2,0,1:T(8,128)(2,1)S(1)} %get-tuple-element.496), channel_id=1, source_target_pairs={{8,0},{16,8},{24,16},{9,1},{17,9},{25,17},{10,2},{18,10},{26,18},{... | collective-permute-start | bytes 393224 | tf_op jit(solution)/shard_map/while/body/eval_jaxpr/ppermute | solution.py:31
  86.9 6.8 %collective-permute-start = (bf16[64,1,64]{0,2,1:T(8,128)(2,1)S(1)}, bf16[64,1,64]{0,2,1:T(8,128)(2,1)S(1)}, u32[]{:S(2)}, u32[]{:S(2)}) collective-permute-start(bf16[64,1,64]{0,2,1:T(8,128)(2,1)S(1)} %get-tuple-element.479), channel_id=1, source_target_pairs={{1,0},{2,1},{3,2},{4,3},{5,4},{6,5},{7,6},{9,8},{10,9},{11,10},{12... | collective-permute-start | bytes 24584 | tf_op jit(solution)/shard_map/while/body/eval_jaxpr/ppermute | solution.py:23
  88.2 6.9 %collective-permute-start.1 = (bf16[64,1,64]{0,2,1:T(8,128)(2,1)S(1)}, bf16[64,1,64]{0,2,1:T(8,128)(2,1)S(1)}, u32[]{:S(2)}, u32[]{:S(2)}) collective-permute-start(bf16[64,1,64]{0,2,1:T(8,128)(2,1)S(1)} %get-tuple-element.480), channel_id=1, source_target_pairs={{0,1},{1,2},{2,3},{3,4},{4,5},{5,6},{6,7},{8,9},{9,10},{10,11},{11... | collective-permute-start | bytes 24584 | tf_op jit(solution)/shard_map/while/body/eval_jaxpr/ppermute | solution.py:20
  100.8 6.8 %collective-permute-start.2 = (bf16[64,1,256]{2,0,1:T(8,128)(2,1)S(1)}, bf16[64,1,256]{2,0,1:T(8,128)(2,1)S(1)}, u32[]{:S(2)}, u32[]{:S(2)}) collective-permute-start(bf16[64,1,256]{2,0,1:T(8,128)(2,1)S(1)} %get-tuple-element.482), channel_id=1, source_target_pairs={{1,0},{2,1},{3,2},{4,3},{5,4},{6,5},{7,6},{9,8},{10,9},{11,10},{12... | collective-permute-start | bytes 98312 | tf_op jit(solution)/shard_map/while/body/eval_jaxpr/ppermute | solution.py:23
  102.1 7.0 %collective-permute-start.3 = (bf16[64,1,256]{2,0,1:T(8,128)(2,1)S(1)}, bf16[64,1,256]{2,0,1:T(8,128)(2,1)S(1)}, u32[]{:S(2)}, u32[]{:S(2)}) collective-permute-start(bf16[64,1,256]{2,0,1:T(8,128)(2,1)S(1)} %get-tuple-element.483), channel_id=1, source_target_pairs={{0,1},{1,2},{2,3},{3,4},{4,5},{5,6},{6,7},{8,9},{9,10},{10,11},{11... | collective-permute-start | bytes 98312 | tf_op jit(solution)/shard_map/while/body/eval_jaxpr/ppermute | solution.py:20
  115.0 5.0 %collective-permute-start.4 = (bf16[64,4,256]{2,0,1:T(8,128)(2,1)S(1)}, bf16[64,4,256]{2,0,1:T(8,128)(2,1)S(1)}, u32[]{:S(2)}, u32[]{:S(2)}) collective-permute-start(bf16[64,4,256]{2,0,1:T(8,128)(2,1)S(1)} %get-tuple-element.496), channel_id=1, source_target_pairs={{8,0},{16,8},{24,16},{9,1},{17,9},{25,17},{10,2},{18,10},{26,18},{... | collective-permute-start | bytes 393224 | tf_op jit(solution)/shard_map/while/body/eval_jaxpr/ppermute | solution.py:31
  120.5 6.8 %collective-permute-start = (bf16[64,1,64]{0,2,1:T(8,128)(2,1)S(1)}, bf16[64,1,64]{0,2,1:T(8,128)(2,1)S(1)}, u32[]{:S(2)}, u32[]{:S(2)}) collective-permute-start(bf16[64,1,64]{0,2,1:T(8,128)(2,1)S(1)} %get-tuple-element.479), channel_id=1, source_target_pairs={{1,0},{2,1},{3,2},{4,3},{5,4},{6,5},{7,6},{9,8},{10,9},{11,10},{12... | collective-permute-start | bytes 24584 | tf_op jit(solution)/shard_map/while/body/eval_jaxpr/ppermute | solution.py:23
  121.8 6.9 %collective-permute-start.1 = (bf16[64,1,64]{0,2,1:T(8,128)(2,1)S(1)}, bf16[64,1,64]{0,2,1:T(8,128)(2,1)S(1)}, u32[]{:S(2)}, u32[]{:S(2)}) collective-permute-start(bf16[64,1,64]{0,2,1:T(8,128)(2,1)S(1)} %get-tuple-element.480), channel_id=1, source_target_pairs={{0,1},{1,2},{2,3},{3,4},{4,5},{5,6},{6,7},{8,9},{9,10},{10,11},{11... | collective-permute-start | bytes 24584 | tf_op jit(solution)/shard_map/while/body/eval_jaxpr/ppermute | solution.py:20
  134.4 6.8 %collective-permute-start.2 = (bf16[64,1,256]{2,0,1:T(8,128)(2,1)S(1)}, bf16[64,1,256]{2,0,1:T(8,128)(2,1)S(1)}, u32[]{:S(2)}, u32[]{:S(2)}) collective-permute-start(bf16[64,1,256]{2,0,1:T(8,128)(2,1)S(1)} %get-tuple-element.482), channel_id=1, source_target_pairs={{1,0},{2,1},{3,2},{4,3},{5,4},{6,5},{7,6},{9,8},{10,9},{11,10},{12... | collective-permute-start | bytes 98312 | tf_op jit(solution)/shard_map/while/body/eval_jaxpr/ppermute | solution.py:23
  135.7 7.0 %collective-permute-start.3 = (bf16[64,1,256]{2,0,1:T(8,128)(2,1)S(1)}, bf16[64,1,256]{2,0,1:T(8,128)(2,1)S(1)}, u32[]{:S(2)}, u32[]{:S(2)}) collective-permute-start(bf16[64,1,256]{2,0,1:T(8,128)(2,1)S(1)} %get-tuple-element.483), channel_id=1, source_target_pairs={{0,1},{1,2},{2,3},{3,4},{4,5},{5,6},{6,7},{8,9},{9,10},{10,11},{11... | collective-permute-start | bytes 98312 | tf_op jit(solution)/shard_map/while/body/eval_jaxpr/ppermute | solution.py:20
  148.6 5.0 %collective-permute-start.4 = (bf16[64,4,256]{2,0,1:T(8,128)(2,1)S(1)}, bf16[64,4,256]{2,0,1:T(8,128)(2,1)S(1)}, u32[]{:S(2)}, u32[]{:S(2)}) collective-permute-start(bf16[64,4,256]{2,0,1:T(8,128)(2,1)S(1)} %get-tuple-element.496), channel_id=1, source_target_pairs={{8,0},{16,8},{24,16},{9,1},{17,9},{25,17},{10,2},{18,10},{26,18},{... | collective-permute-start | bytes 393224 | tf_op jit(solution)/shard_map/while/body/eval_jaxpr/ppermute | solution.py:31
  (8 other events, 31.0 us)
Sparse Core Ops, SparseCore 0:
  167.8 84.6 all-reduce.6
where the time goes:
time: 263 us; the launch traced here: 262 us
  waiting for transfers between devices  110 us (42%)
  starting transfers between devices  65.2 us (25%)
  matrix products  49.5 us (19%)
  between operations  14.6 us (6%)
  other arithmetic  13.4 us (5%)
  local copies, waits for them, and re-layouts  7.91 us (3%)
    psum x1, waiting for transfers between devices, on_device(): lax.psum(fine_local.astype(jnp.bfloat16), 'vol').astype(jnp.float32)  84 us
    ppermute x8, starting transfers between devices, padded_2(): lax.ppermute(lax.slice_in_dim(block, block.shape[dim] - width, None, axis...  42.3 us
    dot_general x216, matrix products, back_sum(): jnp.einsum('io,orp->irp', kernel[tap_key], pieces[tap_key], preferred_ele...  38.6 us
    ppermute x4, waiting for transfers between devices, from_behind(): return lax.ppermute(array, axis, pairs)  12 us
    ppermute x8, waiting for transfers between devices, padded_2(): lax.ppermute(lax.slice_in_dim(block, block.shape[dim] - width, None, axis...  11.6 us
    dot_general x54, matrix products, filter_grid(): jnp.einsum('irp,orp->io', saved_local, pieces[outer_tap, middle_tap, inne...  10.9 us
    ppermute x8, starting transfers between devices, padded_2(): lax.ppermute(lax.slice_in_dim(block, 0, width, axis=dim), axis, backward)  10.3 us
    all_to_all x1, starting transfers between devices, to_depth(): lax.all_to_all(shortened(shaped), 'vol', split_axis=1, concat_axis=2, til...  7.28 us
  transfers between devices with their start and end apart: 22, of which 14 were waited for; matrix products, arithmetic and copies ran while one was open for 2% of the time, Pallas kernels for 0%

commit v1 on v0

v1 whole, which is shorter than its diff:
```python
import functools
import math

import jax
import jax.numpy as jnp
from jax import lax
from jax.experimental import pallas as pl
from jax.experimental.pallas import tpu as pltpu
from jax.sharding import PartitionSpec as P

XL = 16
HX = XL // 2
TAPS = 27
BF = jnp.bfloat16
F32 = jnp.float32


def iota(shape, dim):
    return lax.broadcasted_iota(jnp.int32, shape, dim)


def matmul(a, b):
    return lax.dot_general(a, b, (((1,), (0,)), ((), ())), preferred_element_type=F32)


def matmul_nt(a, b):
    return lax.dot_general(a, b, (((1,), (1,)), ((), ())), preferred_element_type=F32)


def tap_mask(lanes, plane, columns, row_step, col_step):
    lane = iota((1, lanes), 1)
    column = lax.rem(lane, columns) - col_step
    row = lax.div(lax.rem(lane, plane), columns) - row_step
    rows = plane // columns
    inside = (column >= 0) & (column < columns) & (row >= 0) & (row < rows)
    return jnp.where(inside, 1.0, 0.0).astype(BF)


def rolled(value, shift):
    size = value.shape[1]
    shift = shift % size
    return value if shift == 0 else pltpu.roll(value, shift, 1)


def kernel(
    sizes,
    seed, saved, fine_pre, coarse_pre, pooled, fine_w, coarse_w,
    out, fine_all, coarse_all,
    fine_cat, coarse_cat, pre_rows, pool_rows, pre_ext, grad_ext, pool_ext, pool_out,
    coarse_gate, coarse_x, fine_cols, coarse_cols, parts, arrived,
    row_send, row_recv, halo_send, halo_recv, step_send, step_recv, sum_send, sum_recv,
    all_send, all_recv,
):
    segments, n, channels, depth, plane, per, chunks = sizes
    cw = plane // 4
    cdepth = depth // 2
    own = depth * plane
    row_len = coarse_pre.shape[1]
    s = lax.axis_index("segment")
    v = lax.axis_index("vol")
    has_left, has_right = v > 0, v < n - 1
    last = s == segments - 1

    def put(src, dst, send, recv, segment, vol):
        return pltpu.make_async_remote_copy(
            src_ref=src, dst_ref=dst, send_sem=send, recv_sem=recv,
            device_id=(segment, vol), device_id_type=pl.DeviceIdType.MESH,
        )

    barrier = pltpu.get_barrier_semaphore()

    def greet(off, carry):
        pl.semaphore_signal(
            barrier, inc=1, device_id=(s, lax.rem(v + off, n)),
            device_id_type=pl.DeviceIdType.MESH,
        )
        return carry

    lax.fori_loop(1, n, greet, 0)
    for up in (-1, 1):
        for side in (-1, 0, 1):
            there = (s + up >= 0) & (s + up < segments) & (v + side >= 0) & (v + side < n)

            @pl.when(there)
            def _(up=up, side=side):
                pl.semaphore_signal(
                    barrier, inc=1, device_id=(s + up, v + side),
                    device_id_type=pl.DeviceIdType.MESH,
                )

    ups = jnp.where(s > 0, 1, 0) + jnp.where(last, 0, 1)
    sides = 1 + jnp.where(has_left, 1, 0) + jnp.where(has_right, 1, 0)
    pl.semaphore_wait(barrier, n - 1 + ups * sides)

    to_left = put(
        fine_pre.at[:, 0:plane], pre_ext.at[:, plane + own:2 * plane + own],
        halo_send.at[0], halo_recv.at[0], s, v - 1,
    )
    to_right = put(
        fine_pre.at[:, own - plane:own], pre_ext.at[:, 0:plane],
        halo_send.at[1], halo_recv.at[1], s, v + 1,
    )

    def row_copy(which, off):
        src, dst = ((coarse_pre, pre_rows), (pooled, pool_rows))[which]
        return put(
            src, dst.at[v], row_send.at[which, off], row_recv.at[which, v],
            s, lax.rem(v + off, n),
        )

    def send_rows(which):
        def body(off, carry):
            row_copy(which, off).start()
            return carry

        lax.fori_loop(1, n, body, 0)

    def wait_rows(which):
        src, dst = ((coarse_pre, pre_rows), (pooled, pool_rows))[which]

        def body(off, carry):
            u = lax.rem(v + off, n)
            put(src, dst.at[u], row_send.at[which, off], row_recv.at[which, u], s, u).wait_recv()
            return carry

        lax.fori_loop(1, n, body, 0)

    fine_lane = iota((1, own), 1)
    pool_target = (
        lax.div(fine_lane, 2 * plane) * cw
        + lax.div(lax.rem(fine_lane, plane), 2 * XL) * HX
        + lax.div(lax.rem(fine_lane, XL), 2)
    )
    pool_matrix = jnp.where(iota((cdepth * cw, own), 0) == pool_target, 1.0, 0.0).astype(BF)

    def step_copies(src, turn, segment):
        def step(which, a, b, vol):
            return put(a, b, step_send.at[turn, which], step_recv.at[which], segment, vol)

        block = pool_out.at[turn]
        return (
            step(0, src, grad_ext.at[:, plane:plane + own], v),
            step(1, src.at[:, 0:plane], grad_ext.at[:, plane + own:2 * plane + own], v - 1),
            step(2, src.at[:, own - plane:own], grad_ext.at[:, 0:plane], v + 1),
            step(3, block, pool_ext.at[1], v),
            step(4, block, pool_ext.at[2], v - 1),
            step(5, block, pool_ext.at[0], v + 1),
        )

    def guarded(copies, act, with_own):
        if with_own:
            act(copies[3])
            act(copies[0])

        @pl.when(has_left)
        def _():
            act(copies[4])
            act(copies[1])

        @pl.when(has_right)
        def _():
            act(copies[5])
            act(copies[2])

    @pl.when(last)
    def _():
        pool_out[0] = matmul_nt(seed[...], pool_matrix).astype(BF)
        guarded(step_copies(seed, 0, s), lambda c: c.start(), False)
        grad_ext[:, plane:plane + own] = seed[...]
        pool_ext[1] = pool_out[0]

    send_rows(0)

    @pl.when(has_left)
    def _():
        to_left.start()

    @pl.when(has_right)
    def _():
        to_right.start()

    send_rows(1)

    for k in range(TAPS):
        lanes = slice(k * channels, (k + 1) * channels)
        coarse_cat[:, lanes] = coarse_w[k]
        fine_cat[:, lanes] = fine_w[k]
    pre_ext[:, plane:plane + own] = fine_pre[...]
    pre_rows[v] = coarse_pre[...]
    pool_rows[v] = pooled[...]

    @pl.when(v == 0)
    def _():
        pre_ext[:, 0:plane] = jnp.zeros((channels, plane), BF)
        grad_ext[:, 0:plane] = jnp.zeros((channels, plane), BF)
        pool_ext[0] = jnp.zeros(pool_ext.shape[1:], BF)

    @pl.when(v == n - 1)
    def _():
        pre_ext[:, plane + own:2 * plane + own] = jnp.zeros((channels, plane), BF)
        grad_ext[:, plane + own:2 * plane + own] = jnp.zeros((channels, plane), BF)
        pool_ext[2] = jnp.zeros(pool_ext.shape[1:], BF)

    up_lane = iota((1, plane), 1)
    up_target = lax.div(up_lane, 2 * XL) * HX + lax.div(lax.rem(up_lane, XL), 2)
    up_matrix = jnp.where(iota((cw, plane), 0) == up_target, 0.125, 0.0).astype(BF)

    def gathered(rows, first, planes, low, high):
        lane = iota((1, planes * cw), 1)
        slab = lax.div(lane, cw)
        target = (first + slab) * HX + lax.rem(lane, HX)
        target = jnp.where((slab >= low) & (slab < high), target, -1)
        inline = lax.div(lax.rem(lane, cw), HX)
        row = iota((row_len, planes * cw), 0)

        def body(u, total):
            pick = jnp.where(row == jnp.where(inline == u, target, -1), 1.0, 0.0).astype(BF)
            return total + matmul(rows[u], pick)

        return lax.fori_loop(0, n, body, jnp.zeros((channels, planes * cw), F32))

    wait_rows(0)
    reach = cdepth + 4
    coarse_gate[...] = gathered(pre_rows, v * cdepth - 2, reach, 0, reach).astype(BF)

    incoming = step_copies(out, 1, s)

    @pl.when(jnp.logical_not(last))
    def _():
        incoming[3].wait_recv()
        incoming[0].wait_recv()

    @pl.when(has_left)
    def _():
        incoming[5].wait_recv()
        incoming[2].wait_recv()

    @pl.when(has_right)
    def _():
        incoming[4].wait_recv()
        incoming[1].wait_recv()

    side = pool_ext.shape[2]
    near = jnp.concatenate(
        [pool_ext[0][:, side - 2 * cw:], pool_ext[1], pool_ext[2][:, :2 * cw]], axis=1
    )
    coarse_gz = jnp.where(coarse_gate[...] > 0, near, jnp.zeros_like(near))
    wide = (cdepth + 2) * cw
    for row_step in (-1, 0, 1):
        for col_step in (-1, 0, 1):
            mask = tap_mask(wide, cw, HX, row_step, col_step)
            for outer in (-1, 0, 1):
                k = (outer + 1) * 9 + (row_step + 1) * 3 + col_step + 1
                moved = rolled(coarse_gz, outer * cw + row_step * HX + col_step - cw)
                coarse_cols[k * channels:(k + 1) * channels, :] = moved[:, :wide] * mask
    coarse_back = matmul(coarse_cat[...], coarse_cols[...]).astype(BF)

    pieces = []
    for p in range(depth + 2):
        j = (p + 1) // 2
        lanes = slice(p * plane, (p + 1) * plane)
        if p and j == p // 2:
            spread = pieces[-1][1]
        else:
            spread = matmul(coarse_back[:, j * cw:(j + 1) * cw], up_matrix)
        pieces.append((None, spread))

    @pl.when(has_left)
    def _():
        to_right.wait_recv()

    @pl.when(has_right)
    def _():
        to_left.wait_recv()

    gz = []
    for p in range(depth + 2):
        lanes = slice(p * plane, (p + 1) * plane)
        grad = grad_ext[:, lanes].astype(F32) + pieces[p][1]
        gz.append(jnp.where(pre_ext[:, lanes].astype(F32) > 0, grad, 0.0).astype(BF))
    for row_step in (-1, 0, 1):
        for col_step in (-1, 0, 1):
            mask = tap_mask(plane, plane, XL, row_step, col_step)
            r = (row_step + 1) * 3 + col_step + 1
            for p in range(depth + 2):
                fine_cols[r * channels:(r + 1) * channels, p * plane:(p + 1) * plane] = (
                    rolled(gz[p], row_step * XL + col_step) * mask
                )
    group = 9 * channels
    total = grad_ext[:, plane:plane + own].astype(F32)
    for outer in range(3):
        total = total + matmul(
            fine_cat[:, outer * group:(outer + 1) * group],
            fine_cols[:, (2 - outer) * plane:(2 - outer) * plane + own],
        )
    out[...] = total.astype(BF)

    @pl.when(s > 0)
    def _():
        pool_out[1] = matmul_nt(out[...], pool_matrix).astype(BF)
        guarded(step_copies(out, 1, s - 1), lambda c: c.start(), True)

    def place(which, k, value):
        at = (k % per) * channels
        parts[which, k // per, :, at:at + channels] = value

    def chunk_of(which, vol):
        return vol if which == 0 else n - 1 - vol

    def sum_copy(which, off, vol_from, vol_to, chunk):
        return put(
            parts.at[which, chunk], arrived.at[which, vol_from],
            sum_send.at[which, off], sum_recv.at[which, vol_from], s, vol_to,
        )

    def start_sums(which):
        for k in range(TAPS, chunks * per):
            place(which, k, jnp.zeros((channels, channels), BF))

        def body(off, carry):
            t = lax.rem(v + off, n)
            chunk = chunk_of(which, t)

            @pl.when(chunk < chunks)
            def _():
                sum_copy(which, off, v, t, chunk).start()

            return carry

        lax.fori_loop(1, n, body, 0)

    for outer in range(3):
        grads = matmul_nt(
            saved[...], fine_cols[:, (2 - outer) * plane:(2 - outer) * plane + own]
        ).astype(BF)
        for r in range(9):
            place(0, outer * 9 + r, grads[:, r * channels:(r + 1) * channels])
    start_sums(0)

    wait_rows(1)
    coarse_x[...] = gathered(
        pool_rows, v * cdepth - 1, cdepth + 2, 1, 1 + cdepth
    ).astype(BF)
    grads = matmul_nt(coarse_x[...], coarse_cols[...]).astype(BF)
    for k in range(TAPS):
        place(1, k, grads[:, k * channels:(k + 1) * channels])
    start_sums(1)

    collected = (fine_all, coarse_all)

    def all_copy(which, off, chunk, vol_to):
        return put(
            collected[which].at[chunk], collected[which].at[chunk],
            all_send.at[which, off], all_recv.at[which, chunk], s, vol_to,
        )

    for which in (0, 1):
        mine = chunk_of(which, v)

        @pl.when(mine < chunks)
        def _(which=which, mine=mine):
            def add(off, carry):
                u = lax.rem(v + off, n)
                sum_copy(which, off, u, u, mine).wait_recv()
                return carry + arrived[which, u].astype(F32)

            whole = lax.fori_loop(1, n, add, parts[which, mine].astype(F32))
            collected[which][mine] = whole.astype(BF)

            def hand(off, carry):
                all_copy(which, off, mine, lax.rem(v + off, n)).start()
                return carry

            lax.fori_loop(1, n, hand, 0)

    for which in (0, 1):
        mine = chunk_of(which, v)

        def rest(off, carry, which=which, mine=mine):
            t = lax.rem(v + off, n)
            row_copy(which, off).wait_send()
            chunk = chunk_of(which, t)

            @pl.when(chunk < chunks)
            def _():
                sum_copy(which, off, v, t, chunk).wait_send()
                all_copy(which, off, chunk, t).wait_recv()

            @pl.when(mine < chunks)
            def _():
                all_copy(which, off, mine, t).wait_send()

            return carry

        lax.fori_loop(1, n, rest, 0)

    @pl.when(has_left)
    def _():
        to_left.wait_send()

    @pl.when(has_right)
    def _():
        to_right.wait_send()

    @pl.when(last)
    def _():
        guarded(step_copies(seed, 0, s), lambda c: c.wait_send(), False)

    @pl.when(s > 0)
    def _():
        guarded(step_copies(out, 1, s - 1), lambda c: c.wait_send(), True)


def on_device(
    cotangent, labels, class_weight, inputs, fine_pre, pooled, coarse_pre,
    fine_filters, coarse_filters,
):
    segments = lax.axis_size("segment")
    n = lax.axis_size("vol")
    channels, depth, plane = inputs.shape[1:]
    own = depth * plane
    cw = plane // 4
    cdepth = depth // 2
    row_len = pooled.shape[2] * pooled.shape[3]
    per = -(-TAPS // n)
    chunks = -(-TAPS // per)
    cell_weight = jnp.zeros(labels.shape, F32)
    for index in range(class_weight.shape[0]):
        cell_weight = cell_weight + jnp.where(labels == index, class_weight[index], 0.0)
    seed = (cotangent.astype(F32) * cell_weight[None]).astype(BF).reshape(channels, own)
    sizes = (segments, n, channels, depth, plane, per, chunks)
    width = TAPS * channels
    chunk_shape = (channels, per * channels)
    vmem = pl.BlockSpec(memory_space=pltpu.VMEM)
    dma = pltpu.SemaphoreType.DMA
    grad, fine_all, coarse_all = pl.pallas_call(
        functools.partial(kernel, sizes),
        out_shape=(
            jax.ShapeDtypeStruct((channels, own), BF),
            jax.ShapeDtypeStruct((chunks, *chunk_shape), BF),
            jax.ShapeDtypeStruct((chunks, *chunk_shape), BF),
        ),
        in_specs=[vmem] * 7,
        out_specs=(vmem, vmem, vmem),
        scratch_shapes=[
            pltpu.VMEM((channels, width), BF),
            pltpu.VMEM((channels, width), BF),
            pltpu.VMEM((n, channels, row_len), BF),
            pltpu.VMEM((n, channels, row_len), BF),
            pltpu.VMEM((channels, own + 2 * plane), BF),
            pltpu.VMEM((channels, own + 2 * plane), BF),
            pltpu.VMEM((3, channels, cdepth * cw), BF),
            pltpu.VMEM((2, channels, cdepth * cw), BF),
            pltpu.VMEM((channels, (cdepth + 4) * cw), BF),
            pltpu.VMEM((channels, (cdepth + 2) * cw), BF),
            pltpu.VMEM((9 * channels, own + 2 * plane), BF),
            pltpu.VMEM((width, (cdepth + 2) * cw), BF),
            pltpu.VMEM((2, chunks, *chunk_shape), BF),
            pltpu.VMEM((2, n, *chunk_shape), BF),
            dma((2, n)), dma((2, n)), dma((2,)), dma((2,)), dma((2, 6)), dma((6,)),
            dma((2, n)), dma((2, n)), dma((2, n)), dma((2, chunks)),
        ],
        compiler_params=pltpu.CompilerParams(
            collective_id=0, has_side_effects=True, vmem_limit_bytes=60 * 1024 * 1024
        ),
    )(
        seed,
        inputs[0].reshape(channels, own),
        fine_pre[0].reshape(channels, own),
        coarse_pre[0].reshape(channels, row_len),
        pooled[0].reshape(channels, row_len),
        fine_filters[0],
        coarse_filters[0],
    )

    def finish(gathered, cells):
        taps = gathered.reshape(chunks, channels, per, channels).transpose(0, 2, 1, 3)
        taps = taps.reshape(chunks * per, channels, channels)[:TAPS]
        return (taps.astype(F32) * (1.0 / math.sqrt(cells)))[None]

    cells = own * n
    return (
        grad.reshape(1, channels, depth, plane),
        finish(fine_all, cells),
        finish(coarse_all, cells // 8),
    )


def solution(mesh):
    return jax.shard_map(
        on_device,
        mesh=mesh,
        in_specs=(
            P(None, "vol", None),
            P("vol", None),
            P(),
            P("segment", None, "vol", None),
            P("segment", None, "vol", None),
            P("segment", None, "vol", None),
            P("segment", None, "vol", None),
            P("segment", None, None, None),
            P("segment", None, None, None),
        ),
        out_specs=(
            P("segment", None, "vol", None),
            P("segment", None, None, None),
            P("segment", None, None, None),
        ),
        check_vma=False,
    )
```

time: 263 us -> 68.2 us (0.26)
  waiting for transfers between devices: 110 us -> 0 us
  starting transfers between devices: 65.2 us -> 0 us
  Pallas kernels: 0 us -> 54.6 us
  matrix products: 49.5 us -> 0 us
  between operations: 14.6 us -> 0.7 us
  other arithmetic: 13.4 us -> 5.12 us
    psum x1 -> x0, waiting for transfers between devices: 84 us -> none  [on_device(): lax.psum(fine_local.astype(jnp.bfloat16), 'vol').astype(jnp.float32)]
    ppermute x20 -> x0, starting transfers between devices: 57.9 us -> none  [the longest x8 42.3 us: padded_2(): lax.ppermute(lax.slice_in_dim(block, block.shape[dim] - width, None, axis...]
    pallas_call x0 -> x1, Pallas kernels: none -> 54.6 us  [on_device(): pl.pallas_call(functools.partial(kernel, sizes), out_shape=(jax.ShapeDtyp...]
    dot_general x270 -> x0, matrix products: 49.5 us -> none  [the longest x216 38.6 us: back_sum(): jnp.einsum('io,orp->irp', kernel[tap_key], pieces[tap_key], preferred_ele...]
    ppermute x20 -> x0, waiting for transfers between devices: 23.7 us -> none  [the longest x4 12 us: from_behind(): return lax.ppermute(array, axis, pairs)]
    all_to_all x1 -> x0, starting transfers between devices: 7.28 us -> none  [to_depth(): lax.all_to_all(shortened(shaped), 'vol', split_axis=1, concat_axis=2, til...]
    select_n x18 -> x0, other arithmetic: 3.28 us -> none  [the longest x5 2.6 us: plane_shift(): return jnp.where(inside, shifted, jnp.zeros_like(shifted))]
    unnamed x14 -> x13, local copies, waits for them, and re-layouts: 1.05 us -> 3.9 us
  transfers between devices with their start and end apart: 22 -> 0, of which waited for: 14 -> 0; matrix products, arithmetic and copies ran while one was open for 2% -> 0% of each run, Pallas kernels for 0% -> 0%
where the time goes in v1:
time: 68.2 us; the launch traced here: 67.9 us
  Pallas kernels  54.6 us (80%)
  local copies, waits for them, and re-layouts  7.46 us (11%)
  other arithmetic  5.12 us (8%)
  between operations  0.7 us (1%)
    pallas_call x1, Pallas kernels, on_device(): pl.pallas_call(functools.partial(kernel, sizes), out_shape=(jax.ShapeDtyp...  54.6 us
    unnamed x13, local copies, waits for them, and re-layouts  3.9 us
    broadcast_in_dim x2, other arithmetic, finish(): return (taps.astype(F32) * (1.0 / math.sqrt(cells)))[None]  2.02 us
    add x1, other arithmetic, on_device(): cell_weight + jnp.where(labels == index, class_weight[index], 0.0)  1.94 us
    reshape x1, local copies, waits for them, and re-layouts, on_device(): grad.reshape(1, channels, depth, plane)  1.68 us

profile of v1, /device:TPU:0, one launch (start us, length us, event | category | flops | bytes accessed | tf_op | source)
XLA Modules:
  0.0 67.9 jit_solution(9227231855919622565)
XLA Ops:
  0.6 0.0 copy-start.3
  0.6 0.6 copy-done.3
  1.3 0.6 fusion.2
  1.9 0.0 copy-start.4
  1.9 0.7 %copy-done.4 = s32[4,256]{1,0:T(4,128)S(1)} copy-done((s32[4,256]{1,0:T(4,128)S(1)}, s32[4,256]{1,0:T(4,128)}, u32[]{:S(2)}) %copy-start.4) | copy-done | bytes 4120
  2.6 1.9 %select_add_fusion = f32[4,256]{1,0:T(4,128)S(1)} fusion(s32[4,256]{1,0:T(4,128)S(1)} %copy-done.4, f32[]{:T(128)} %bitcast.2, f32[]{:T(128)} %bitcast.1, f32[]{:T(128)} %bitcast), kind=kLoop, calls=%fused_computation.5 | loop fusion | flops 8192 | bytes 8204 | tf_op jit(solution)/shard_map/add | solution.py:429
  4.5 1.0 %multiply_convert_fusion = bf16[64,4,256]{2,1,0:T(4,128)(2,1)S(1)} fusion(bf16[64,4,256]{2,1,0:T(4,128)(2,1)} %param.9, f32[4,256]{1,0:T(4,128)S(1)} %select_add_fusion), kind=kLoop, calls=%fused_computation.4 | loop fusion | flops 196608 | bytes 266240 | tf_op jit(solution)/shard_map/convert_element_type | solution.py:430
  5.5 0.0 copy-start.1
  5.5 0.7 copy.12
  6.2 0.3 copy-done.1
  6.4 0.0 copy-start.2
  6.4 0.7 copy.13
  7.1 0.3 copy-done.2
  7.4 0.7 copy.14
  8.1 54.6 %shard_map.112 = (bf16[64,1024]{1,0:T(8,128)(2,1)}, bf16[7,64,256]{2,1,0:T(8,128)(2,1)}, bf16[7,64,256]{2,1,0:T(8,128)(2,1)}) custom-call(bf16[64,1024]{1,0:T(8,128)(2,1)} %bitcast.23, bf16[64,1024]{1,0:T(8,128)(2,1)} %bitcast.24, bf16[64,1024]{1,0:T(8,128)(2,1)} %bitcast.25, bf16[64,128]{1,0:T(8,128)(2,1)} %bitcast.31, bf16[64,128]{1,0:T(8,128)(2,1)} %bitcast.32, ...), custom_call_target="tpu_custom_call" | custom-call | tf_op jit(solution)/shard_map/pallas_call | solution.py:436
  62.7 0.0 copy-start
  62.7 1.7 %reshape.22 = bf16[1,64,4,256]{3,2,1,0:T(4,128)(2,1)} reshape(bf16[64,1024]{1,0:T(8,128)(2,1)} %get-tuple-element.6) | data formatting | bytes 262144 | tf_op jit(solution)/shard_map/reshape | solution.py:483
  64.4 0.0 copy-done
  64.4 1.3 %fusion = (bf16[7,64,64]{2,1,0:T(8,128)(2,1)S(1)}, bf16[7,64,64]{2,1,0:T(8,128)(2,1)S(1)}, bf16[7,64,64]{2,1,0:T(8,128)(2,1)S(1)}, bf16[7,64,64]{2,1,0:T(8,128)(...) fusion(bf16[7,64,256]{2,1,0:T(8,128)(2,1)} %get-tuple-element.8, ...), kind=kLoop, calls=%fused_computation.6 | loop fusion | bytes 917504 | tf_op jit(solution)/shard_map/slice.4
  65.7 0.1 pad_maximum_fusion.1
  65.8 1.0 %multiply_bitcast_fusion = f32[1,27,64,64]{3,2,1,0:T(8,128)} fusion(bf16[28,64,64]{2,1,0:T(8,128)(2,1)S(1)} %bitcast.21), kind=kLoop, calls=%fused_computation | loop fusion | flops 221184 | bytes 663552 | tf_op jit(solution)/shard_map/broadcast_in_dim | solution.py:479
  66.8 0.1 pad_maximum_fusion
  66.9 1.0 %multiply_bitcast_fusion.1 = f32[1,27,64,64]{3,2,1,0:T(8,128)} fusion(bf16[28,64,64]{2,1,0:T(8,128)(2,1)S(1)} %bitcast.22), kind=kLoop, calls=%fused_computation.1 | loop fusion | flops 221184 | bytes 663552 | tf_op jit(solution)/shard_map/broadcast_in_dim | solution.py:479
Async XLA Ops:
  0.6 0.7 copy-start.3
  1.9 0.7 %copy-start.4 = (s32[4,256]{1,0:T(4,128)S(1)}, s32[4,256]{1,0:T(4,128)}, u32[]{:S(2)}) copy-start(s32[4,256]{1,0:T(4,128)} %param.10) | copy-start | bytes 12292
  5.5 1.0 %copy-start.1 = (bf16[1,64,4,256]{3,2,1,0:T(4,128)(2,1)S(1)}, bf16[1,64,4,256]{3,2,1,0:T(4,128)(2,1)}, u32[]{:S(2)}) copy-start(bf16[1,64,4,256]{3,2,1,0:T(4,128)(2,1)} %param.12) | copy-start | bytes 393220
  6.4 1.0 %copy-start.2 = (bf16[1,64,4,256]{3,2,1,0:T(4,128)(2,1)S(1)}, bf16[1,64,4,256]{3,2,1,0:T(4,128)(2,1)}, u32[]{:S(2)}) copy-start(bf16[1,64,4,256]{3,2,1,0:T(4,128)(2,1)} %param.13) | copy-start | bytes 393220
  62.7 1.7 %copy-start = (bf16[7,64,256]{2,1,0:T(8,128)(2,1)S(1)}, bf16[7,64,256]{2,1,0:T(8,128)(2,1)}, u32[]{:S(2)}) copy-start(bf16[7,64,256]{2,1,0:T(8,128)(2,1)} %get-tuple-element.7) | copy-start | bytes 688132

commit v2 on v1

--- a/solution.py
+++ b/solution.py
@@ -44,14 +44,14 @@
 
 def kernel(
     sizes,
-    seed, saved, fine_pre, coarse_pre, pooled, fine_w, coarse_w,
-    out, fine_all, coarse_all,
-    fine_cat, coarse_cat, pre_rows, pool_rows, pre_ext, grad_ext, pool_ext, pool_out,
+    class_weight, cotangent, labels, saved, fine_pre, coarse_pre, pooled, fine_w, coarse_w,
+    out, fine_out, coarse_out,
+    seed, collected, fine_cat, coarse_cat, pre_rows, pool_rows, pre_ext, grad_ext, pool_ext, pool_out,
     coarse_gate, coarse_x, fine_cols, coarse_cols, parts, arrived,
     row_send, row_recv, halo_send, halo_recv, step_send, step_recv, sum_send, sum_recv,
-    all_send, all_recv,
+    all_send, all_recv, turn_sem,
 ):
-    segments, n, channels, depth, plane, per, chunks = sizes
+    segments, n, channels, depth, plane, per, chunks, scales = sizes
     cw = plane // 4
     cdepth = depth // 2
     own = depth * plane
@@ -93,11 +93,11 @@
     pl.semaphore_wait(barrier, n - 1 + ups * sides)
 
     to_left = put(
-        fine_pre.at[:, 0:plane], pre_ext.at[:, plane + own:2 * plane + own],
+        fine_pre.at[0], pre_ext.at[depth + 1],
         halo_send.at[0], halo_recv.at[0], s, v - 1,
     )
     to_right = put(
-        fine_pre.at[:, own - plane:own], pre_ext.at[:, 0:plane],
+        fine_pre.at[depth - 1], pre_ext.at[0],
         halo_send.at[1], halo_recv.at[1], s, v + 1,
     )
 
@@ -139,66 +139,93 @@
 
         block = pool_out.at[turn]
         return (
-            step(0, src, grad_ext.at[:, plane:plane + own], v),
-            step(1, src.at[:, 0:plane], grad_ext.at[:, plane + own:2 * plane + own], v - 1),
-            step(2, src.at[:, own - plane:own], grad_ext.at[:, 0:plane], v + 1),
+            step(0, src, grad_ext.at[1:depth + 1], v),
+            step(1, src.at[0], grad_ext.at[depth + 1], v - 1),
+            step(2, src.at[depth - 1], grad_ext.at[0], v + 1),
             step(3, block, pool_ext.at[1], v),
             step(4, block, pool_ext.at[2], v - 1),
             step(5, block, pool_ext.at[0], v + 1),
         )
 
     def guarded(copies, act, with_own):
+        @pl.when(has_left)
+        def _():
+            act(copies[4])
+
+        @pl.when(has_right)
+        def _():
+            act(copies[5])
+
         if with_own:
             act(copies[3])
+
+        @pl.when(has_left)
+        def _():
+            act(copies[1])
+
+        @pl.when(has_right)
+        def _():
+            act(copies[2])
+
+        if with_own:
             act(copies[0])
 
+    def joined(ref):
+        return jnp.concatenate([ref[p] for p in range(depth)], axis=1)
+
+    def send_saved():
+        send_rows(0)
+
         @pl.when(has_left)
         def _():
-            act(copies[4])
-            act(copies[1])
+            to_left.start()
 
         @pl.when(has_right)
         def _():
-            act(copies[5])
-            act(copies[2])
+            to_right.start()
 
     @pl.when(last)
     def _():
-        pool_out[0] = matmul_nt(seed[...], pool_matrix).astype(BF)
+        send_rows(0)
+        for p in range(depth):
+            label = labels[p:p + 1, :]
+            weight = jnp.zeros(label.shape, F32)
+            for index in range(class_weight.shape[0]):
+                weight = weight + jnp.where(label == index, class_weight[index], 0.0)
+            block = (cotangent[p].astype(F32) * weight).astype(BF)
+            seed[p] = block
+            grad_ext[p + 1] = block
+        pool_out[0] = matmul_nt(joined(seed), pool_matrix).astype(BF)
         guarded(step_copies(seed, 0, s), lambda c: c.start(), False)
-        grad_ext[:, plane:plane + own] = seed[...]
         pool_ext[1] = pool_out[0]
 
-    send_rows(0)
-
-    @pl.when(has_left)
-    def _():
-        to_left.start()
-
-    @pl.when(has_right)
-    def _():
-        to_right.start()
-
-    send_rows(1)
+        @pl.when(has_left)
+        def _():
+            to_left.start()
+
+        @pl.when(has_right)
+        def _():
+            to_right.start()
 
     for k in range(TAPS):
         lanes = slice(k * channels, (k + 1) * channels)
         coarse_cat[:, lanes] = coarse_w[k]
         fine_cat[:, lanes] = fine_w[k]
-    pre_ext[:, plane:plane + own] = fine_pre[...]
+    for p in range(depth):
+        pre_ext[p + 1] = fine_pre[p]
     pre_rows[v] = coarse_pre[...]
     pool_rows[v] = pooled[...]
 
     @pl.when(v == 0)
     def _():
-        pre_ext[:, 0:plane] = jnp.zeros((channels, plane), BF)
-        grad_ext[:, 0:plane] = jnp.zeros((channels, plane), BF)
+        pre_ext[0] = jnp.zeros((channels, plane), BF)
+        grad_ext[0] = jnp.zeros((channels, plane), BF)
         pool_ext[0] = jnp.zeros(pool_ext.shape[1:], BF)
 
     @pl.when(v == n - 1)
     def _():
-        pre_ext[:, plane + own:2 * plane + own] = jnp.zeros((channels, plane), BF)
-        grad_ext[:, plane + own:2 * plane + own] = jnp.zeros((channels, plane), BF)
+        pre_ext[depth + 1] = jnp.zeros((channels, plane), BF)
+        grad_ext[depth + 1] = jnp.zeros((channels, plane), BF)
         pool_ext[2] = jnp.zeros(pool_ext.shape[1:], BF)
 
     up_lane = iota((1, plane), 1)
@@ -219,26 +246,94 @@
 
         return lax.fori_loop(0, n, body, jnp.zeros((channels, planes * cw), F32))
 
+    @pl.when(jnp.logical_not(last))
+    def _():
+        pl.semaphore_wait(turn_sem, 1)
+        send_saved()
+
     wait_rows(0)
+
+    @pl.when(s > 0)
+    def _():
+        pl.semaphore_signal(
+            turn_sem, inc=1, device_id=(s - 1, v), device_id_type=pl.DeviceIdType.MESH
+        )
+
+    send_rows(1)
     reach = cdepth + 4
     coarse_gate[...] = gathered(pre_rows, v * cdepth - 2, reach, 0, reach).astype(BF)
 
+    def take_pooled():
+        wait_rows(1)
+        coarse_x[...] = gathered(
+            pool_rows, v * cdepth - 1, cdepth + 2, 1, 1 + cdepth
+        ).astype(BF)
+
+    @pl.when(jnp.logical_not(last))
+    def _():
+        take_pooled()
+
     incoming = step_copies(out, 1, s)
 
-    @pl.when(jnp.logical_not(last))
-    def _():
-        incoming[3].wait_recv()
-        incoming[0].wait_recv()
-
-    @pl.when(has_left)
-    def _():
-        incoming[5].wait_recv()
-        incoming[2].wait_recv()
-
-    @pl.when(has_right)
-    def _():
-        incoming[4].wait_recv()
-        incoming[1].wait_recv()
+    def wait_incoming(middle, left, right):
+        @pl.when(jnp.logical_not(last))
+        def _():
+            incoming[middle].wait_recv()
+
+        @pl.when(has_left)
+        def _():
+            incoming[left].wait_recv()
+
+        @pl.when(has_right)
+        def _():
+            incoming[right].wait_recv()
+
+    wait_incoming(3, 5, 4)
+
+    def place(which, k, value):
+        at = (k % per) * channels
+        parts[which, k // per, :, at:at + channels] = value
+
+    def chunk_of(which, vol):
+        return vol if which == 0 else n - 1 - vol
+
+    def sum_copy(which, off, vol_from, vol_to, chunk):
+        return put(
+            parts.at[which, chunk], arrived.at[which, vol_from],
+            sum_send.at[which, off], sum_recv.at[which, vol_from], s, vol_to,
+        )
+
+    def start_sums(which):
+        for k in range(TAPS, chunks * per):
+            place(which, k, jnp.zeros((channels, channels), BF))
+
+        def body(off, carry):
+            t = lax.rem(v + off, n)
+            chunk = chunk_of(which, t)
+
+            @pl.when(chunk < chunks)
+            def _():
+                sum_copy(which, off, v, t, chunk).start()
+
+            return carry
+
+        lax.fori_loop(1, n, body, 0)
+
+    def fine_sums():
+        rows = joined(saved)
+        for outer in range(3):
+            grads = matmul_nt(
+                rows, fine_cols[:, (2 - outer) * plane:(2 - outer) * plane + own]
+            ).astype(BF)
+            for r in range(9):
+                place(0, outer * 9 + r, grads[:, r * channels:(r + 1) * channels])
+        start_sums(0)
+
+    def coarse_sums():
+        grads = matmul_nt(coarse_x[...], coarse_cols[...]).astype(BF)
+        for k in range(TAPS):
+            place(1, k, grads[:, k * channels:(k + 1) * channels])
+        start_sums(1)
 
     side = pool_ext.shape[2]
     near = jnp.concatenate(
@@ -253,17 +348,20 @@
                 k = (outer + 1) * 9 + (row_step + 1) * 3 + col_step + 1
                 moved = rolled(coarse_gz, outer * cw + row_step * HX + col_step - cw)
                 coarse_cols[k * channels:(k + 1) * channels, :] = moved[:, :wide] * mask
+    @pl.when(s == 0)
+    def _():
+        coarse_sums()
+
     coarse_back = matmul(coarse_cat[...], coarse_cols[...]).astype(BF)
 
     pieces = []
     for p in range(depth + 2):
         j = (p + 1) // 2
-        lanes = slice(p * plane, (p + 1) * plane)
         if p and j == p // 2:
-            spread = pieces[-1][1]
+            spread = pieces[-1]
         else:
             spread = matmul(coarse_back[:, j * cw:(j + 1) * cw], up_matrix)
-        pieces.append((None, spread))
+        pieces.append(spread)
 
     @pl.when(has_left)
     def _():
@@ -273,11 +371,11 @@
     def _():
         to_left.wait_recv()
 
+    wait_incoming(0, 2, 1)
     gz = []
     for p in range(depth + 2):
-        lanes = slice(p * plane, (p + 1) * plane)
-        grad = grad_ext[:, lanes].astype(F32) + pieces[p][1]
-        gz.append(jnp.where(pre_ext[:, lanes].astype(F32) > 0, grad, 0.0).astype(BF))
+        grad = grad_ext[p].astype(F32) + pieces[p]
+        gz.append(jnp.where(pre_ext[p].astype(F32) > 0, grad, 0.0).astype(BF))
     for row_step in (-1, 0, 1):
         for col_step in (-1, 0, 1):
             mask = tap_mask(plane, plane, XL, row_step, col_step)
@@ -286,75 +384,42 @@
                 fine_cols[r * channels:(r + 1) * channels, p * plane:(p + 1) * plane] = (
                     rolled(gz[p], row_step * XL + col_step) * mask
                 )
+    @pl.when(s == 0)
+    def _():
+        fine_sums()
+
     group = 9 * channels
-    total = grad_ext[:, plane:plane + own].astype(F32)
+    total = jnp.concatenate([grad_ext[p + 1].astype(F32) for p in range(depth)], axis=1)
     for outer in range(3):
         total = total + matmul(
             fine_cat[:, outer * group:(outer + 1) * group],
             fine_cols[:, (2 - outer) * plane:(2 - outer) * plane + own],
         )
-    out[...] = total.astype(BF)
+    for p in range(depth):
+        out[p] = total[:, p * plane:(p + 1) * plane].astype(BF)
 
     @pl.when(s > 0)
     def _():
-        pool_out[1] = matmul_nt(out[...], pool_matrix).astype(BF)
+        pool_out[1] = matmul_nt(joined(out), pool_matrix).astype(BF)
         guarded(step_copies(out, 1, s - 1), lambda c: c.start(), True)
 
-    def place(which, k, value):
-        at = (k % per) * channels
-        parts[which, k // per, :, at:at + channels] = value
-
-    def chunk_of(which, vol):
-        return vol if which == 0 else n - 1 - vol
-
-    def sum_copy(which, off, vol_from, vol_to, chunk):
-        return put(
-            parts.at[which, chunk], arrived.at[which, vol_from],
-            sum_send.at[which, off], sum_recv.at[which, vol_from], s, vol_to,
-        )
-
-    def start_sums(which):
-        for k in range(TAPS, chunks * per):
-            place(which, k, jnp.zeros((channels, channels), BF))
-
-        def body(off, carry):
-            t = lax.rem(v + off, n)
-            chunk = chunk_of(which, t)
-
-            @pl.when(chunk < chunks)
-            def _():
-                sum_copy(which, off, v, t, chunk).start()
-
-            return carry
-
-        lax.fori_loop(1, n, body, 0)
-
-    for outer in range(3):
-        grads = matmul_nt(
-            saved[...], fine_cols[:, (2 - outer) * plane:(2 - outer) * plane + own]
-        ).astype(BF)
-        for r in range(9):
-            place(0, outer * 9 + r, grads[:, r * channels:(r + 1) * channels])
-    start_sums(0)
-
-    wait_rows(1)
-    coarse_x[...] = gathered(
-        pool_rows, v * cdepth - 1, cdepth + 2, 1, 1 + cdepth
-    ).astype(BF)
-    grads = matmul_nt(coarse_x[...], coarse_cols[...]).astype(BF)
-    for k in range(TAPS):
-        place(1, k, grads[:, k * channels:(k + 1) * channels])
-    start_sums(1)
-
-    collected = (fine_all, coarse_all)
+    @pl.when(s > 0)
+    def _():
+        fine_sums()
+
+        @pl.when(last)
+        def _():
+            take_pooled()
+
+        coarse_sums()
 
     def all_copy(which, off, chunk, vol_to):
         return put(
-            collected[which].at[chunk], collected[which].at[chunk],
+            collected.at[which, chunk], collected.at[which, chunk],
             all_send.at[which, off], all_recv.at[which, chunk], s, vol_to,
         )
 
-    for which in (0, 1):
+    for which in (1, 0):
         mine = chunk_of(which, v)
 
         @pl.when(mine < chunks)
@@ -365,13 +430,24 @@
                 return carry + arrived[which, u].astype(F32)
 
             whole = lax.fori_loop(1, n, add, parts[which, mine].astype(F32))
-            collected[which][mine] = whole.astype(BF)
+            collected[which, mine] = whole.astype(BF)
 
             def hand(off, carry):
                 all_copy(which, off, mine, lax.rem(v + off, n)).start()
                 return carry
 
             lax.fori_loop(1, n, hand, 0)
+
+    for which in (1, 0):
+        ref, scale = ((fine_out, scales[0]), (coarse_out, scales[1]))[which]
+        for chunk in range(chunks):
+            @pl.when(chunk_of(which, v) != chunk)
+            def _(which=which, chunk=chunk):
+                all_copy(which, 1, chunk, v).wait_recv()
+
+            for k in range(chunk * per, min(TAPS, (chunk + 1) * per)):
+                at = (k % per) * channels
+                ref[k] = collected[which, chunk, :, at:at + channels].astype(F32) * scale
 
     for which in (0, 1):
         mine = chunk_of(which, v)
@@ -384,7 +460,6 @@
             @pl.when(chunk < chunks)
             def _():
                 sum_copy(which, off, v, t, chunk).wait_send()
-                all_copy(which, off, chunk, t).wait_recv()
 
             @pl.when(mine < chunks)
             def _():
@@ -424,31 +499,31 @@
     row_len = pooled.shape[2] * pooled.shape[3]
     per = -(-TAPS // n)
     chunks = -(-TAPS // per)
-    cell_weight = jnp.zeros(labels.shape, F32)
-    for index in range(class_weight.shape[0]):
-        cell_weight = cell_weight + jnp.where(labels == index, class_weight[index], 0.0)
-    seed = (cotangent.astype(F32) * cell_weight[None]).astype(BF).reshape(channels, own)
-    sizes = (segments, n, channels, depth, plane, per, chunks)
+    cells = own * n
+    scales = (1.0 / math.sqrt(cells), 1.0 / math.sqrt(cells // 8))
+    sizes = (segments, n, channels, depth, plane, per, chunks, scales)
     width = TAPS * channels
     chunk_shape = (channels, per * channels)
     vmem = pl.BlockSpec(memory_space=pltpu.VMEM)
     dma = pltpu.SemaphoreType.DMA
-    grad, fine_all, coarse_all = pl.pallas_call(
+    grad, fine_grads, coarse_grads = pl.pallas_call(
         functools.partial(kernel, sizes),
         out_shape=(
-            jax.ShapeDtypeStruct((channels, own), BF),
-            jax.ShapeDtypeStruct((chunks, *chunk_shape), BF),
-            jax.ShapeDtypeStruct((chunks, *chunk_shape), BF),
+            jax.ShapeDtypeStruct((depth, channels, plane), BF),
+            jax.ShapeDtypeStruct((TAPS, channels, channels), F32),
+            jax.ShapeDtypeStruct((TAPS, channels, channels), F32),
         ),
-        in_specs=[vmem] * 7,
+        in_specs=[pl.BlockSpec(memory_space=pltpu.SMEM)] + [vmem] * 8,
         out_specs=(vmem, vmem, vmem),
         scratch_shapes=[
+            pltpu.VMEM((depth, channels, plane), BF),
+            pltpu.VMEM((2, chunks, *chunk_shape), BF),
             pltpu.VMEM((channels, width), BF),
             pltpu.VMEM((channels, width), BF),
             pltpu.VMEM((n, channels, row_len), BF),
             pltpu.VMEM((n, channels, row_len), BF),
-            pltpu.VMEM((channels, own + 2 * plane), BF),
-            pltpu.VMEM((channels, own + 2 * plane), BF),
+            pltpu.VMEM((depth + 2, channels, plane), BF),
+            pltpu.VMEM((depth + 2, channels, plane), BF),
             pltpu.VMEM((3, channels, cdepth * cw), BF),
             pltpu.VMEM((2, channels, cdepth * cw), BF),
             pltpu.VMEM((channels, (cdepth + 4) * cw), BF),
@@ -459,31 +534,24 @@
             pltpu.VMEM((2, n, *chunk_shape), BF),
             dma((2, n)), dma((2, n)), dma((2,)), dma((2,)), dma((2, 6)), dma((6,)),
             dma((2, n)), dma((2, n)), dma((2, n)), dma((2, chunks)),
+            pltpu.SemaphoreType.REGULAR,
         ],
         compiler_params=pltpu.CompilerParams(
             collective_id=0, has_side_effects=True, vmem_limit_bytes=60 * 1024 * 1024
         ),
     )(
-        seed,
-        inputs[0].reshape(channels, own),
-        fine_pre[0].reshape(channels, own),
+        class_weight,
+        cotangent.transpose(1, 0, 2),
+        labels,
+        inputs[0].transpose(1, 0, 2),
+        fine_pre[0].transpose(1, 0, 2),
         coarse_pre[0].reshape(channels, row_len),
         pooled[0].reshape(channels, row_len),
         fine_filters[0],
         coarse_filters[0],
     )
 
-    def finish(gathered, cells):
-        taps = gathered.reshape(chunks, channels, per, channels).transpose(0, 2, 1, 3)
-        taps = taps.reshape(chunks * per, channels, channels)[:TAPS]
-        return (taps.astype(F32) * (1.0 / math.sqrt(cells)))[None]
-
-    cells = own * n
-    return (
-        grad.reshape(1, channels, depth, plane),
-        finish(fine_all, cells),
-        finish(coarse_all, cells // 8),
-    )
+    return (grad.transpose(1, 0, 2)[None], fine_grads[None], coarse_grads[None])
 
 
 def solution(mesh):

time: 68.2 us -> 67.4 us (0.988)
  other arithmetic: 5.12 us -> 0 us
  Pallas kernels: 54.6 us -> 59.4 us
    pallas_call x1, Pallas kernels: 54.6 us -> 59.4 us  [on_device(): pl.pallas_call(functools.partial(kernel, sizes), out_shape=(jax.ShapeDtyp...]
    unnamed x13 -> x10, local copies, waits for them, and re-layouts: 3.9 us -> 6.46 us
    broadcast_in_dim x2 -> x0, other arithmetic: 2.02 us -> none  [finish(): return (taps.astype(F32) * (1.0 / math.sqrt(cells)))[None]]
    add x1 -> x0, other arithmetic: 1.94 us -> none  [on_device(): cell_weight + jnp.where(labels == index, class_weight[index], 0.0)]
    reshape x1 -> x0, local copies, waits for them, and re-layouts: 1.68 us -> none  [on_device(): grad.reshape(1, channels, depth, plane)]
    another operation x1 -> x0, local copies, waits for them, and re-layouts: 1.3 us -> none
    convert_element_type x1 -> x0, other arithmetic: 0.96 us -> none  [on_device(): (cotangent.astype(F32) * cell_weight[None]).astype(BF)]
    transpose x0 -> x1, local copies, waits for them, and re-layouts: none -> 0.73 us  [on_device(): fine_pre[0].transpose(1, 0, 2)]
where the time goes in v2:
time: 67.4 us; the launch traced here: 67.2 us
  Pallas kernels  59.4 us (88%)
  local copies, waits for them, and re-layouts  7.18 us (11%)
    pallas_call x1, Pallas kernels, on_device(): pl.pallas_call(functools.partial(kernel, sizes), out_shape=(jax.ShapeDtyp...  59.4 us
    unnamed x10, local copies, waits for them, and re-layouts  6.46 us

profile of v2, /device:TPU:0, one launch (start us, length us, event | category | flops | bytes accessed | tf_op | source)
XLA Modules:
  0.0 67.2 jit_solution(10899037212186421786)
XLA Ops:
  0.6 0.0 copy-start.1
  0.6 0.0 copy-start.2
  0.7 1.6 %copy.19 = bf16[64,4,256]{2,0,1:T(8,128)(2,1)} copy(bf16[64,4,256]{2,1,0:T(4,128)(2,1)} %param.9) | data formatting | bytes 262144 | tf_op args[0]
  2.3 0.0 copy-done.1
  2.3 0.0 copy-done.2
  2.3 0.7 %copy_bitcast_fusion = (bf16[4,64,256]{2,1,0:T(8,128)(2,1)}, bf16[4,64,256]{2,1,0:T(8,128)(2,1)}) fusion(bf16[1,64,4,256]{3,2,1,0:T(4,128)(2,1)S(1)} %copy-done.1, bf16[1,64,4,256]{3,2,1,0:T(4,128)(2,1)S(1)} %copy-done.2), kind=kLoop, calls=%fused_computation | loop fusion | bytes 524288 | tf_op jit(solution)/shard_map/transpose | solution.py:547
  3.0 59.4 %shard_map.112 = (bf16[4,64,256]{2,1,0:T(8,128)(2,1)}, f32[27,64,64]{2,1,0:T(8,128)}, f32[27,64,64]{2,1,0:T(8,128)}) custom-call(f32[3]{0:T(128)} %class_weight.1, bf16[4,64,256]{2,1,0:T(8,128)(2,1)} %bitcast.22, s32[4,256]{1,0:T(4,128)} %labels.1, bf16[4,64,256]{2,1,0:T(8,128)(2,1)} %get-tuple-element.13.saved, ...), custom_call_target="tpu_custom_call" | custom-call | tf_op jit(solution)/shard_map/pallas_call | solution.py:509
  62.4 1.7 %copy.15 = bf16[1,64,4,256]{3,2,1,0:T(4,128)(2,1)} copy(bf16[1,64,4,256]{3,1,2,0:T(8,128)(2,1)} %bitcast.25) | data formatting | bytes 262144
  64.0 0.0 copy-start
  64.0 2.3 %copy.22 = f32[1,27,64,64]{3,2,1,0:T(8,128)} copy(f32[1,27,64,64]{3,2,1,0:T(8,128)} %bitcast.21) | data formatting | bytes 884736
  66.3 0.0 copy-done
  66.3 0.9 %copy.23 = f32[1,27,64,64]{3,2,1,0:T(8,128)} copy(f32[1,27,64,64]{3,2,1,0:T(8,128)S(1)} %bitcast.20) | data formatting | bytes 884736
Async XLA Ops:
  0.6 1.6 %copy-start.1 = (bf16[1,64,4,256]{3,2,1,0:T(4,128)(2,1)S(1)}, bf16[1,64,4,256]{3,2,1,0:T(4,128)(2,1)}, u32[]{:S(2)}) copy-start(bf16[1,64,4,256]{3,2,1,0:T(4,128)(2,1)} %param.13) | copy-start | bytes 393220
  0.6 1.6 %copy-start.2 = (bf16[1,64,4,256]{3,2,1,0:T(4,128)(2,1)S(1)}, bf16[1,64,4,256]{3,2,1,0:T(4,128)(2,1)}, u32[]{:S(2)}) copy-start(bf16[1,64,4,256]{3,2,1,0:T(4,128)(2,1)} %param.12) | copy-start | bytes 393220
  64.0 2.3 %copy-start = (f32[27,64,64]{2,1,0:T(8,128)S(1)}, f32[27,64,64]{2,1,0:T(8,128)}, u32[]{:S(2)}) copy-start(f32[27,64,64]{2,1,0:T(8,128)} %get-tuple-element.8) | copy-start | bytes 1327108

commit v3 on v2

--- a/solution.py
+++ b/solution.py
@@ -45,13 +45,13 @@
 def kernel(
     sizes,
     class_weight, cotangent, labels, saved, fine_pre, coarse_pre, pooled, fine_w, coarse_w,
-    out, fine_out, coarse_out,
-    seed, collected, fine_cat, coarse_cat, pre_rows, pool_rows, pre_ext, grad_ext, pool_ext, pool_out,
+    out, collected,
+    seed, fine_cat, coarse_cat, pre_rows, pool_rows, pre_ext, grad_ext, pool_ext, pool_out,
     coarse_gate, coarse_x, fine_cols, coarse_cols, parts, arrived,
     row_send, row_recv, halo_send, halo_recv, step_send, step_recv, sum_send, sum_recv,
-    all_send, all_recv, turn_sem,
+    all_send, all_recv,
 ):
-    segments, n, channels, depth, plane, per, chunks, scales = sizes
+    segments, n, channels, depth, plane, per, chunks = sizes
     cw = plane // 4
     cdepth = depth // 2
     own = depth * plane
@@ -173,20 +173,10 @@
     def joined(ref):
         return jnp.concatenate([ref[p] for p in range(depth)], axis=1)
 
-    def send_saved():
-        send_rows(0)
-
-        @pl.when(has_left)
-        def _():
-            to_left.start()
-
-        @pl.when(has_right)
-        def _():
-            to_right.start()
+    send_rows(0)
 
     @pl.when(last)
     def _():
-        send_rows(0)
         for p in range(depth):
             label = labels[p:p + 1, :]
             weight = jnp.zeros(label.shape, F32)
@@ -199,13 +189,13 @@
         guarded(step_copies(seed, 0, s), lambda c: c.start(), False)
         pool_ext[1] = pool_out[0]
 
-        @pl.when(has_left)
-        def _():
-            to_left.start()
-
-        @pl.when(has_right)
-        def _():
-            to_right.start()
+    @pl.when(has_left)
+    def _():
+        to_left.start()
+
+    @pl.when(has_right)
+    def _():
+        to_right.start()
 
     for k in range(TAPS):
         lanes = slice(k * channels, (k + 1) * channels)
@@ -246,19 +236,7 @@
 
         return lax.fori_loop(0, n, body, jnp.zeros((channels, planes * cw), F32))
 
-    @pl.when(jnp.logical_not(last))
-    def _():
-        pl.semaphore_wait(turn_sem, 1)
-        send_saved()
-
     wait_rows(0)
-
-    @pl.when(s > 0)
-    def _():
-        pl.semaphore_signal(
-            turn_sem, inc=1, device_id=(s - 1, v), device_id_type=pl.DeviceIdType.MESH
-        )
-
     send_rows(1)
     reach = cdepth + 4
     coarse_gate[...] = gathered(pre_rows, v * cdepth - 2, reach, 0, reach).astype(BF)
@@ -438,17 +416,6 @@
 
             lax.fori_loop(1, n, hand, 0)
 
-    for which in (1, 0):
-        ref, scale = ((fine_out, scales[0]), (coarse_out, scales[1]))[which]
-        for chunk in range(chunks):
-            @pl.when(chunk_of(which, v) != chunk)
-            def _(which=which, chunk=chunk):
-                all_copy(which, 1, chunk, v).wait_recv()
-
-            for k in range(chunk * per, min(TAPS, (chunk + 1) * per)):
-                at = (k % per) * channels
-                ref[k] = collected[which, chunk, :, at:at + channels].astype(F32) * scale
-
     for which in (0, 1):
         mine = chunk_of(which, v)
 
@@ -460,6 +427,7 @@
             @pl.when(chunk < chunks)
             def _():
                 sum_copy(which, off, v, t, chunk).wait_send()
+                all_copy(which, off, chunk, t).wait_recv()
 
             @pl.when(mine < chunks)
             def _():
@@ -484,6 +452,15 @@
     @pl.when(s > 0)
     def _():
         guarded(step_copies(out, 1, s - 1), lambda c: c.wait_send(), True)
+
+
+def finish(per, scales, collected, fine_out, coarse_out):
+    channels = fine_out.shape[1]
+    for which, ref in enumerate((fine_out, coarse_out)):
+        for k in range(TAPS):
+            at = (k % per) * channels
+            value = collected[which, k // per, :, at:at + channels]
+            ref[k] = value.astype(F32) * scales[which]
 
 
 def on_device(
@@ -501,23 +478,21 @@
     chunks = -(-TAPS // per)
     cells = own * n
     scales = (1.0 / math.sqrt(cells), 1.0 / math.sqrt(cells // 8))
-    sizes = (segments, n, channels, depth, plane, per, chunks, scales)
+    sizes = (segments, n, channels, depth, plane, per, chunks)
     width = TAPS * channels
     chunk_shape = (channels, per * channels)
     vmem = pl.BlockSpec(memory_space=pltpu.VMEM)
     dma = pltpu.SemaphoreType.DMA
-    grad, fine_grads, coarse_grads = pl.pallas_call(
+    grad, collected = pl.pallas_call(
         functools.partial(kernel, sizes),
         out_shape=(
             jax.ShapeDtypeStruct((depth, channels, plane), BF),
-            jax.ShapeDtypeStruct((TAPS, channels, channels), F32),
-            jax.ShapeDtypeStruct((TAPS, channels, channels), F32),
+            jax.ShapeDtypeStruct((2, chunks, *chunk_shape), BF),
         ),
         in_specs=[pl.BlockSpec(memory_space=pltpu.SMEM)] + [vmem] * 8,
-        out_specs=(vmem, vmem, vmem),
+        out_specs=(vmem, vmem),
         scratch_shapes=[
             pltpu.VMEM((depth, channels, plane), BF),
-            pltpu.VMEM((2, chunks, *chunk_shape), BF),
             pltpu.VMEM((channels, width), BF),
             pltpu.VMEM((channels, width), BF),
             pltpu.VMEM((n, channels, row_len), BF),
@@ -534,7 +509,6 @@
             pltpu.VMEM((2, n, *chunk_shape), BF),
             dma((2, n)), dma((2, n)), dma((2,)), dma((2,)), dma((2, 6)), dma((6,)),
             dma((2, n)), dma((2, n)), dma((2, n)), dma((2, chunks)),
-            pltpu.SemaphoreType.REGULAR,
         ],
         compiler_params=pltpu.CompilerParams(
             collective_id=0, has_side_effects=True, vmem_limit_bytes=60 * 1024 * 1024
@@ -551,6 +525,13 @@
         coarse_filters[0],
     )
 
+    tap_shape = jax.ShapeDtypeStruct((TAPS, channels, channels), F32)
+    fine_grads, coarse_grads = pl.pallas_call(
+        functools.partial(finish, per, scales),
+        out_shape=(tap_shape, tap_shape),
+        in_specs=[vmem],
+        out_specs=(vmem, vmem),
+    )(collected)
     return (grad.transpose(1, 0, 2)[None], fine_grads[None], coarse_grads[None])
 
 

time: 67.4 us -> 60.2 us (0.89)
  Pallas kernels: 59.4 us -> 55.3 us
  local copies, waits for them, and re-layouts: 7.18 us -> 4.02 us
    pallas_call x1, Pallas kernels: 59.4 us -> 52.8 us  [on_device(): pl.pallas_call(functools.partial(kernel, sizes), out_shape=(jax.ShapeDtyp...]
    unnamed x10 -> x6, local copies, waits for them, and re-layouts: 6.46 us -> 3.29 us
    pallas_call x0 -> x1, Pallas kernels: none -> 2.47 us  [on_device(): pl.pallas_call(functools.partial(finish, per, scales), out_shape=(tap_sha...]
where the time goes in v3:
time: 60.2 us; the launch traced here: 59.9 us
  Pallas kernels  55.3 us (92%)
  local copies, waits for them, and re-layouts  4.02 us (7%)
  between operations  0.66 us (1%)
    pallas_call x1, Pallas kernels, on_device(): pl.pallas_call(functools.partial(kernel, sizes), out_shape=(jax.ShapeDtyp...  52.8 us
    unnamed x6, local copies, waits for them, and re-layouts  3.29 us
    pallas_call x1, Pallas kernels, on_device(): pl.pallas_call(functools.partial(finish, per, scales), out_shape=(tap_sha...  2.47 us

profile of v3, /device:TPU:0, one launch (start us, length us, event | category | flops | bytes accessed | tf_op | source)
XLA Modules:
  0.0 59.9 jit_solution(5595544072682969518)
XLA Ops:
  0.6 0.0 copy-start
  0.6 0.0 copy-start.1
  0.7 1.6 %copy.19 = bf16[64,4,256]{2,0,1:T(8,128)(2,1)} copy(bf16[64,4,256]{2,1,0:T(4,128)(2,1)} %param.9) | data formatting | bytes 262144 | tf_op args[0]
  2.3 0.0 copy-done
  2.3 0.0 copy-done.1
  2.3 0.7 %copy_bitcast_fusion = (bf16[4,64,256]{2,1,0:T(8,128)(2,1)}, bf16[4,64,256]{2,1,0:T(8,128)(2,1)}) fusion(bf16[1,64,4,256]{3,2,1,0:T(4,128)(2,1)S(1)} %copy-done, bf16[1,64,4,256]{3,2,1,0:T(4,128)(2,1)S(1)} %copy-done.1), kind=kLoop, calls=%fused_computation | loop fusion | bytes 524288 | tf_op jit(solution)/shard_map/transpose | solution.py:521
  3.0 52.8 %shard_map.112 = (bf16[4,64,256]{2,1,0:T(8,128)(2,1)}, bf16[2,7,64,256]{3,2,1,0:T(8,128)(2,1)}) custom-call(f32[3]{0:T(128)} %class_weight.1, bf16[4,64,256]{2,1,0:T(8,128)(2,1)} %bitcast.20, s32[4,256]{1,0:T(4,128)} %labels.1, bf16[4,64,256]{2,1,0:T(8,128)(2,1)} %get-tuple-element.15.saved, bf16[4,64,256]{2,1,0:T(8,128)(2,1)} %get-tuple-element.14.fine_pre, ...), custom_call_target="tpu_custom_call" | custom-call | tf_op jit(solution)/shard_map/pallas_call | solution.py:486
  55.8 1.7 %copy.15 = bf16[1,64,4,256]{3,2,1,0:T(4,128)(2,1)} copy(bf16[1,64,4,256]{3,1,2,0:T(8,128)(2,1)} %bitcast.23) | data formatting | bytes 262144
  57.5 2.5 %shard_map.113 = (f32[27,64,64]{2,1,0:T(8,128)}, f32[27,64,64]{2,1,0:T(8,128)}) custom-call(bf16[2,7,64,256]{3,2,1,0:T(8,128)(2,1)} %get-tuple-element.8.collected), custom_call_target="tpu_custom_call" | custom-call | tf_op jit(solution)/shard_map/pallas_call | solution.py:529
Async XLA Ops:
  0.6 1.6 %copy-start = (bf16[1,64,4,256]{3,2,1,0:T(4,128)(2,1)S(1)}, bf16[1,64,4,256]{3,2,1,0:T(4,128)(2,1)}, u32[]{:S(2)}) copy-start(bf16[1,64,4,256]{3,2,1,0:T(4,128)(2,1)} %param.13) | copy-start | bytes 393220
  0.6 1.6 %copy-start.1 = (bf16[1,64,4,256]{3,2,1,0:T(4,128)(2,1)S(1)}, bf16[1,64,4,256]{3,2,1,0:T(4,128)(2,1)}, u32[]{:S(2)}) copy-start(bf16[1,64,4,256]{3,2,1,0:T(4,128)(2,1)} %param.12) | copy-start | bytes 393220

commit v4 on v3

--- a/solution.py
+++ b/solution.py
@@ -47,7 +47,7 @@
     class_weight, cotangent, labels, saved, fine_pre, coarse_pre, pooled, fine_w, coarse_w,
     out, collected,
     seed, fine_cat, coarse_cat, pre_rows, pool_rows, pre_ext, grad_ext, pool_ext, pool_out,
-    coarse_gate, coarse_x, fine_cols, coarse_cols, parts, arrived,
+    coarse_gate, fine_x, coarse_x, fine_cols, coarse_cols, parts, arrived,
     row_send, row_recv, halo_send, halo_recv, step_send, step_recv, sum_send, sum_recv,
     all_send, all_recv,
 ):
@@ -198,9 +198,16 @@
         to_right.start()
 
     for k in range(TAPS):
-        lanes = slice(k * channels, (k + 1) * channels)
-        coarse_cat[:, lanes] = coarse_w[k]
-        fine_cat[:, lanes] = fine_w[k]
+        rows = slice(k // 9 * channels, (k // 9 + 1) * channels)
+        lanes = slice(k % 9 * channels, (k % 9 + 1) * channels)
+        coarse_cat[rows, lanes] = coarse_w[k]
+        fine_cat[rows, lanes] = fine_w[k]
+    for outer in range(3):
+        rows = slice(outer * channels, (outer + 1) * channels)
+        for p in range(depth + 2):
+            q = p - 2 + outer
+            block = saved[q] if 0 <= q < depth else jnp.zeros((channels, plane), BF)
+            fine_x[rows, p * plane:(p + 1) * plane] = block
     for p in range(depth):
         pre_ext[p + 1] = fine_pre[p]
     pre_rows[v] = coarse_pre[...]
@@ -243,9 +250,9 @@
 
     def take_pooled():
         wait_rows(1)
-        coarse_x[...] = gathered(
-            pool_rows, v * cdepth - 1, cdepth + 2, 1, 1 + cdepth
-        ).astype(BF)
+        own_x = gathered(pool_rows, v * cdepth - 2, reach, 2, 2 + cdepth).astype(BF)
+        for outer in range(3):
+            coarse_x[outer * channels:(outer + 1) * channels, :] = rolled(own_x, (1 - outer) * cw)
 
     @pl.when(jnp.logical_not(last))
     def _():
@@ -297,40 +304,43 @@
 
         lax.fori_loop(1, n, body, 0)
 
+    def place_all(which, grads):
+        for k in range(TAPS):
+            rows = slice(k // 9 * channels, (k // 9 + 1) * channels)
+            place(which, k, grads[rows, k % 9 * channels:(k % 9 + 1) * channels])
+        start_sums(which)
+
     def fine_sums():
-        rows = joined(saved)
-        for outer in range(3):
-            grads = matmul_nt(
-                rows, fine_cols[:, (2 - outer) * plane:(2 - outer) * plane + own]
-            ).astype(BF)
-            for r in range(9):
-                place(0, outer * 9 + r, grads[:, r * channels:(r + 1) * channels])
-        start_sums(0)
+        place_all(0, matmul_nt(fine_x[...], fine_cols[...]).astype(BF))
 
     def coarse_sums():
-        grads = matmul_nt(coarse_x[...], coarse_cols[...]).astype(BF)
-        for k in range(TAPS):
-            place(1, k, grads[:, k * channels:(k + 1) * channels])
-        start_sums(1)
+        place_all(1, matmul_nt(coarse_x[...], coarse_cols[...]).astype(BF))
 
     side = pool_ext.shape[2]
     near = jnp.concatenate(
         [pool_ext[0][:, side - 2 * cw:], pool_ext[1], pool_ext[2][:, :2 * cw]], axis=1
     )
     coarse_gz = jnp.where(coarse_gate[...] > 0, near, jnp.zeros_like(near))
-    wide = (cdepth + 2) * cw
     for row_step in (-1, 0, 1):
         for col_step in (-1, 0, 1):
-            mask = tap_mask(wide, cw, HX, row_step, col_step)
-            for outer in (-1, 0, 1):
-                k = (outer + 1) * 9 + (row_step + 1) * 3 + col_step + 1
-                moved = rolled(coarse_gz, outer * cw + row_step * HX + col_step - cw)
-                coarse_cols[k * channels:(k + 1) * channels, :] = moved[:, :wide] * mask
+            mask = tap_mask(reach * cw, cw, HX, row_step, col_step)
+            r = (row_step + 1) * 3 + col_step + 1
+            coarse_cols[r * channels:(r + 1) * channels, :] = (
+                rolled(coarse_gz, row_step * HX + col_step) * mask
+            )
+
     @pl.when(s == 0)
     def _():
         coarse_sums()
 
-    coarse_back = matmul(coarse_cat[...], coarse_cols[...]).astype(BF)
+    def over_depth(terms, step, width):
+        return sum(
+            terms[outer * channels:(outer + 1) * channels, (2 - outer) * step:(2 - outer) * step + width]
+            for outer in range(3)
+        )
+
+    terms = matmul(coarse_cat[...], coarse_cols[...])
+    coarse_back = over_depth(terms, cw, (cdepth + 2) * cw).astype(BF)
 
     pieces = []
     for p in range(depth + 2):
@@ -366,13 +376,8 @@
     def _():
         fine_sums()
 
-    group = 9 * channels
-    total = jnp.concatenate([grad_ext[p + 1].astype(F32) for p in range(depth)], axis=1)
-    for outer in range(3):
-        total = total + matmul(
-            fine_cat[:, outer * group:(outer + 1) * group],
-            fine_cols[:, (2 - outer) * plane:(2 - outer) * plane + own],
-        )
+    total = over_depth(matmul(fine_cat[...], fine_cols[...]), plane, own)
+    total = total + jnp.concatenate([grad_ext[p + 1].astype(F32) for p in range(depth)], axis=1)
     for p in range(depth):
         out[p] = total[:, p * plane:(p + 1) * plane].astype(BF)
 
@@ -479,7 +484,6 @@
     cells = own * n
     scales = (1.0 / math.sqrt(cells), 1.0 / math.sqrt(cells // 8))
     sizes = (segments, n, channels, depth, plane, per, chunks)
-    width = TAPS * channels
     chunk_shape = (channels, per * channels)
     vmem = pl.BlockSpec(memory_space=pltpu.VMEM)
     dma = pltpu.SemaphoreType.DMA
@@ -493,8 +497,8 @@
         out_specs=(vmem, vmem),
         scratch_shapes=[
             pltpu.VMEM((depth, channels, plane), BF),
-            pltpu.VMEM((channels, width), BF),
-            pltpu.VMEM((channels, width), BF),
+            pltpu.VMEM((3 * channels, 9 * channels), BF),
+            pltpu.VMEM((3 * channels, 9 * channels), BF),
             pltpu.VMEM((n, channels, row_len), BF),
             pltpu.VMEM((n, channels, row_len), BF),
             pltpu.VMEM((depth + 2, channels, plane), BF),
@@ -502,9 +506,10 @@
             pltpu.VMEM((3, channels, cdepth * cw), BF),
             pltpu.VMEM((2, channels, cdepth * cw), BF),
             pltpu.VMEM((channels, (cdepth + 4) * cw), BF),
-            pltpu.VMEM((channels, (cdepth + 2) * cw), BF),
+            pltpu.VMEM((3 * channels, own + 2 * plane), BF),
+            pltpu.VMEM((3 * channels, (cdepth + 4) * cw), BF),
             pltpu.VMEM((9 * channels, own + 2 * plane), BF),
-            pltpu.VMEM((width, (cdepth + 2) * cw), BF),
+            pltpu.VMEM((9 * channels, (cdepth + 4) * cw), BF),
             pltpu.VMEM((2, chunks, *chunk_shape), BF),
             pltpu.VMEM((2, n, *chunk_shape), BF),
             dma((2, n)), dma((2, n)), dma((2,)), dma((2,)), dma((2, 6)), dma((6,)),

time: 60.2 us -> 59.6 us (0.990)
    pallas_call x1, Pallas kernels: 52.8 us -> 52.2 us  [on_device(): pl.pallas_call(functools.partial(kernel, sizes), out_shape=(jax.ShapeDtyp...]
where the time goes in v4:
time: 59.6 us; the launch traced here: 59.3 us
  Pallas kernels  54.7 us (92%)
  local copies, waits for them, and re-layouts  4.02 us (7%)
  between operations  0.66 us (1%)
    pallas_call x1, Pallas kernels, on_device(): pl.pallas_call(functools.partial(kernel, sizes), out_shape=(jax.ShapeDtyp...  52.2 us
    unnamed x6, local copies, waits for them, and re-layouts  3.29 us
    pallas_call x1, Pallas kernels, on_device(): pl.pallas_call(functools.partial(finish, per, scales), out_shape=(tap_sha...  2.47 us

profile of v4, /device:TPU:0, one launch (start us, length us, event | category | flops | bytes accessed | tf_op | source)
XLA Modules:
  0.0 59.3 jit_solution(9971808228901428487)
XLA Ops:
  0.6 0.0 copy-start
  0.6 0.0 copy-start.1
  0.7 1.6 %copy.19 = bf16[64,4,256]{2,0,1:T(8,128)(2,1)} copy(bf16[64,4,256]{2,1,0:T(4,128)(2,1)} %param.9) | data formatting | bytes 262144 | tf_op args[0]
  2.3 0.0 copy-done
  2.3 0.0 copy-done.1
  2.3 0.7 %copy_bitcast_fusion = (bf16[4,64,256]{2,1,0:T(8,128)(2,1)}, bf16[4,64,256]{2,1,0:T(8,128)(2,1)}) fusion(bf16[1,64,4,256]{3,2,1,0:T(4,128)(2,1)S(1)} %copy-done, bf16[1,64,4,256]{3,2,1,0:T(4,128)(2,1)S(1)} %copy-done.1), kind=kLoop, calls=%fused_computation | loop fusion | bytes 524288 | tf_op jit(solution)/shard_map/transpose | solution.py:526
  3.0 52.2 %shard_map.112 = (bf16[4,64,256]{2,1,0:T(8,128)(2,1)}, bf16[2,7,64,256]{3,2,1,0:T(8,128)(2,1)}) custom-call(f32[3]{0:T(128)} %class_weight.1, bf16[4,64,256]{2,1,0:T(8,128)(2,1)} %bitcast.20, s32[4,256]{1,0:T(4,128)} %labels.1, bf16[4,64,256]{2,1,0:T(8,128)(2,1)} %get-tuple-element.15.saved, bf16[4,64,256]{2,1,0:T(8,128)(2,1)} %get-tuple-element.14.fine_pre, ...), custom_call_target="tpu_custom_call" | custom-call | tf_op jit(solution)/shard_map/pallas_call | solution.py:490
  55.2 1.7 %copy.15 = bf16[1,64,4,256]{3,2,1,0:T(4,128)(2,1)} copy(bf16[1,64,4,256]{3,1,2,0:T(8,128)(2,1)} %bitcast.23) | data formatting | bytes 262144
  56.9 2.5 %shard_map.113 = (f32[27,64,64]{2,1,0:T(8,128)}, f32[27,64,64]{2,1,0:T(8,128)}) custom-call(bf16[2,7,64,256]{3,2,1,0:T(8,128)(2,1)} %get-tuple-element.8.collected), custom_call_target="tpu_custom_call" | custom-call | tf_op jit(solution)/shard_map/pallas_call | solution.py:534
Async XLA Ops:
  0.6 1.6 %copy-start = (bf16[1,64,4,256]{3,2,1,0:T(4,128)(2,1)S(1)}, bf16[1,64,4,256]{3,2,1,0:T(4,128)(2,1)}, u32[]{:S(2)}) copy-start(bf16[1,64,4,256]{3,2,1,0:T(4,128)(2,1)} %param.13) | copy-start | bytes 393220
  0.6 1.6 %copy-start.1 = (bf16[1,64,4,256]{3,2,1,0:T(4,128)(2,1)S(1)}, bf16[1,64,4,256]{3,2,1,0:T(4,128)(2,1)}, u32[]{:S(2)}) copy-start(bf16[1,64,4,256]{3,2,1,0:T(4,128)(2,1)} %param.12) | copy-start | bytes 393220

commit v5 on v4

--- a/solution.py
+++ b/solution.py
@@ -93,11 +93,11 @@
     pl.semaphore_wait(barrier, n - 1 + ups * sides)
 
     to_left = put(
-        fine_pre.at[0], pre_ext.at[depth + 1],
+        pre_ext.at[1], pre_ext.at[depth + 1],
         halo_send.at[0], halo_recv.at[0], s, v - 1,
     )
     to_right = put(
-        fine_pre.at[depth - 1], pre_ext.at[0],
+        pre_ext.at[depth], pre_ext.at[0],
         halo_send.at[1], halo_recv.at[1], s, v + 1,
     )
 
@@ -177,18 +177,21 @@
 
     @pl.when(last)
     def _():
+        planes = jnp.swapaxes(cotangent[...], 0, 1)
         for p in range(depth):
             label = labels[p:p + 1, :]
             weight = jnp.zeros(label.shape, F32)
             for index in range(class_weight.shape[0]):
                 weight = weight + jnp.where(label == index, class_weight[index], 0.0)
-            block = (cotangent[p].astype(F32) * weight).astype(BF)
+            block = (planes[p].astype(F32) * weight).astype(BF)
             seed[p] = block
             grad_ext[p + 1] = block
         pool_out[0] = matmul_nt(joined(seed), pool_matrix).astype(BF)
         guarded(step_copies(seed, 0, s), lambda c: c.start(), False)
         pool_ext[1] = pool_out[0]
 
+    pre_ext[1:depth + 1] = jnp.swapaxes(fine_pre[...], 0, 1)
+
     @pl.when(has_left)
     def _():
         to_left.start()
@@ -202,14 +205,13 @@
         lanes = slice(k % 9 * channels, (k % 9 + 1) * channels)
         coarse_cat[rows, lanes] = coarse_w[k]
         fine_cat[rows, lanes] = fine_w[k]
+    planes = jnp.swapaxes(saved[...], 0, 1)
     for outer in range(3):
         rows = slice(outer * channels, (outer + 1) * channels)
         for p in range(depth + 2):
             q = p - 2 + outer
-            block = saved[q] if 0 <= q < depth else jnp.zeros((channels, plane), BF)
+            block = planes[q] if 0 <= q < depth else jnp.zeros((channels, plane), BF)
             fine_x[rows, p * plane:(p + 1) * plane] = block
-    for p in range(depth):
-        pre_ext[p + 1] = fine_pre[p]
     pre_rows[v] = coarse_pre[...]
     pool_rows[v] = pooled[...]
 
@@ -459,8 +461,9 @@
         guarded(step_copies(out, 1, s - 1), lambda c: c.wait_send(), True)
 
 
-def finish(per, scales, collected, fine_out, coarse_out):
+def finish(per, scales, grad, collected, grad_out, fine_out, coarse_out):
     channels = fine_out.shape[1]
+    grad_out[...] = jnp.swapaxes(grad[...], 0, 1)
     for which, ref in enumerate((fine_out, coarse_out)):
         for k in range(TAPS):
             at = (k % per) * channels
@@ -520,10 +523,10 @@
         ),
     )(
         class_weight,
-        cotangent.transpose(1, 0, 2),
+        cotangent,
         labels,
-        inputs[0].transpose(1, 0, 2),
-        fine_pre[0].transpose(1, 0, 2),
+        inputs[0],
+        fine_pre[0],
         coarse_pre[0].reshape(channels, row_len),
         pooled[0].reshape(channels, row_len),
         fine_filters[0],
@@ -531,13 +534,13 @@
     )
 
     tap_shape = jax.ShapeDtypeStruct((TAPS, channels, channels), F32)
-    fine_grads, coarse_grads = pl.pallas_call(
+    grad, fine_grads, coarse_grads = pl.pallas_call(
         functools.partial(finish, per, scales),
-        out_shape=(tap_shape, tap_shape),
-        in_specs=[vmem],
-        out_specs=(vmem, vmem),
-    )(collected)
-    return (grad.transpose(1, 0, 2)[None], fine_grads[None], coarse_grads[None])
+        out_shape=(jax.ShapeDtypeStruct((channels, depth, plane), BF), tap_shape, tap_shape),
+        in_specs=[vmem] * 2,
+        out_specs=(vmem, vmem, vmem),
+    )(grad, collected)
+    return (grad[None], fine_grads[None], coarse_grads[None])
 
 
 def solution(mesh):

time: 59.6 us -> 55.5 us (0.931)
  local copies, waits for them, and re-layouts: 4.02 us -> 0 us
    unnamed x6 -> x0, local copies, waits for them, and re-layouts: 3.29 us -> none
    transpose x1 -> x0, local copies, waits for them, and re-layouts: 0.73 us -> none  [on_device(): fine_pre[0].transpose(1, 0, 2)]
where the time goes in v5:
time: 55.5 us; the launch traced here: 55.4 us
  Pallas kernels  54.7 us (99%)
  between operations  0.64 us (1%)
    pallas_call x1, Pallas kernels, on_device(): pl.pallas_call(functools.partial(kernel, sizes), out_shape=(jax.ShapeDtyp...  52.1 us
    pallas_call x1, Pallas kernels, on_device(): pl.pallas_call(functools.partial(finish, per, scales), out_shape=(jax.Sha...  2.59 us

profile of v5, /device:TPU:0, one launch (start us, length us, event | category | flops | bytes accessed | tf_op | source)
XLA Modules:
  0.0 55.4 jit_solution(2715700117356044433)
XLA Ops:
  0.6 52.1 %shard_map.112 = (bf16[4,64,256]{2,1,0:T(8,128)(2,1)}, bf16[2,7,64,256]{3,2,1,0:T(8,128)(2,1)}) custom-call(f32[3]{0:T(128)} %class_weight.1, bf16[64,4,256]{2,1,0:T(4,128)(2,1)} %cotangent.1, s32[4,256]{1,0:T(4,128)} %labels.1, bf16[64,4,256]{2,1,0:T(4,128)(2,1)} %bitcast.11, bf16[64,4,256]{2,1,0:T(4,128)(2,1)} %bitcast.12, bf16[64,128]{1,0:T(8,128)(2,1)} %bitcast.13, ...), custom_call_target="tpu_custom_call" | custom-call | tf_op jit(solution)/shard_map/pallas_call | solution.py:493
  52.8 2.6 %shard_map.113 = (bf16[64,4,256]{2,1,0:T(4,128)(2,1)}, f32[27,64,64]{2,1,0:T(8,128)}, f32[27,64,64]{2,1,0:T(8,128)}) custom-call(bf16[4,64,256]{2,1,0:T(8,128)(2,1)} %get-tuple-element.8.grad, bf16[2,7,64,256]{3,2,1,0:T(8,128)(2,1)} %get-tuple-element.9.collected), custom_call_target="tpu_custom_call" | custom-call | tf_op jit(solution)/shard_map/pallas_call | solution.py:537
